TPU v7x, 768 devices: a whole 4x8x12 slice. The times are simulated.
768 devices in a mesh: dp: 12 (over z_lo, core), enc: 64 (over z_hi, y, x).
Axes of the slice: x: 4, y: 8, z: 12 (z_hi: 2, z_lo: 6; z = z_hi * 6 + z_lo), core: 2. Of those that a mesh axis runs over, the one named last changes fastest.
Arguments:
- counts: int32 [12, 64], P('dp'), may hold values from 1 to 48, 1536 in all within a row
- pixels: bfloat16 [12, 49152, 392], P('dp', 'enc'), may hold values from -6 to 6
- cotangent: bfloat16 [12, 24576, 1728], P('dp', 'enc'), may hold values from -0.03125 to 0.03125
Outputs:
- grad_patch: float32 [1728, 392], P('enc')
Inputs may be any that keep to these rules, and one draw needn't show every extreme that they name: `counts`: each row of a group sums to exactly 1536; in each row some device holds exactly 48 live blocks.
All inputs are finite; a program needn't handle non-finite values.
Results may differ from a plain program's by a relative error of at most 0.0003.
Values may be sent and summed in bfloat16 or wider, within the bound.
No kernel may reach another device: no remote copies, remote signals or barrier semaphores. Data moves between devices by JAX's collectives and lax.ppermute only.
A program may use at most 32 MiB of HBM per device.

v0:
```python
import jax
import jax.numpy as jnp
from jax import lax
from jax.sharding import Mesh
from jax.sharding import PartitionSpec as P

BLK = 16
ENC = ("enc_0", "enc_1", "enc_2")


def sum_in_order(blocks, axes, turns):
    inside = blocks.shape[1:]
    blocks = blocks.reshape(*(lax.axis_size(a) for a in axes), *inside)
    blocks = jnp.moveaxis(blocks, turns, range(len(axes))).reshape(-1, *inside)
    for k in turns:
        blocks = lax.psum_scatter(blocks, axes[k], scatter_dimension=0, tiled=True)
    return blocks[0]


def cut_along(value, dim, devices):
    before, after = (value.shape[:dim], value.shape[dim + 1 :])
    return jnp.moveaxis(value.reshape(*before, devices, -1, *after), dim, 0)


def scatter_axes(value, axes, turns, dim):
    devices = lax.axis_size(axes)
    return sum_in_order(cut_along(value, dim, devices), axes, turns)


def copy_for_each(value, axis):
    copies = jnp.broadcast_to(value, (lax.axis_size(axis), *value.shape))
    return lax.all_to_all(copies, axis, split_axis=0, concat_axis=0, tiled=True)


def taken_together(value, axis):
    everything = copy_for_each(value, axis)
    return jnp.sum(everything, axis=0)


def lookup(table, index, peers):
    return jnp.sum(jnp.where(index[:, None] == peers[None, :], table[None, :], 0), axis=1)


def per_device(counts, pixels, cotangent):
    n_enc = lax.axis_size(ENC)
    me_enc = lax.axis_index(ENC)
    group_counts = counts[0]
    starts = jnp.cumsum(group_counts) - group_counts
    peers = jnp.arange(n_enc, dtype=jnp.int32)
    own_count = jnp.sum(jnp.where(peers == me_enc, group_counts, 0))
    own_start = jnp.sum(jnp.where(peers == me_enc, starts, 0))
    slots = pixels.shape[1] // BLK
    width = pixels.shape[2]
    per_peer = max(1, slots // n_enc)
    slot_ids = jnp.arange(slots, dtype=jnp.int32)
    global_ids = own_start + slot_ids
    target = global_ids % n_enc * per_peer + slot_ids // n_enc
    columns = jnp.arange(n_enc * per_peer, dtype=jnp.int32)
    select = (columns[:, None] == target[None, :]) & (slot_ids < own_count)[None, :]
    blocks = pixels[0].reshape(slots, BLK * width)
    outgoing = jnp.dot(
        select.astype(jnp.bfloat16), blocks, preferred_element_type=jnp.float32
    ).astype(jnp.bfloat16)
    arrived = lax.all_to_all(outgoing, ENC, split_axis=0, concat_axis=0, tiled=True)
    source = columns // per_peer
    rank = columns % per_peer
    src_start = lookup(starts, source, peers)
    src_count = lookup(group_counts, source, peers)
    first_slot = (me_enc - src_start) % n_enc
    slot_there = first_slot + rank * n_enc
    valid = slot_there < src_count
    compact = (src_start + slot_there) // n_enc
    own_blocks = cotangent.shape[1] // BLK
    compact_ids = jnp.arange(own_blocks, dtype=jnp.int32)
    order = (compact_ids[:, None] == compact[None, :]) & valid[None, :]
    owned = jnp.dot(order.astype(jnp.bfloat16), arrived, preferred_element_type=jnp.float32).astype(
        jnp.bfloat16
    )
    owned = owned.reshape(own_blocks * BLK, width)
    cot_rows = cotangent[0]
    local = scatter_axes(
        lax.dot_general(
            cot_rows, owned, (((0,), (0,)), ((), ())), preferred_element_type=jnp.float32
        ),
        ENC,
        (2, 1, 0),
        0,
    )
    return taken_together(local, "dp")


def solution(mesh):
    torus = Mesh(mesh.devices.reshape(mesh.shape["dp"], 2, 8, 4), ("dp", "enc_0", "enc_1", "enc_2"))
    return jax.shard_map(
        per_device,
        mesh=torus,
        in_specs=(P("dp", None), P("dp", ENC, None), P("dp", ENC, None)),
        out_specs=P(ENC, None),
        check_vma=False,
    )
```

profile of v0, /device:TPU:1, one launch (start us, length us, event | category | flops | bytes accessed | tf_op | source)
XLA Modules:
  0.0 339.5 jit_solution(15603663518421303603)
XLA Ops:
  6.5 0.0 copy-start
  6.5 0.8 copy.19
  7.4 0.1 reduce-window.4
  7.5 0.1 reduce
  7.6 1.4 fusion.14
  9.0 0.7 fusion.12
  9.7 0.7 iota_compare_fusion.3
  10.3 1.3 copy.20
  11.7 0.9 reshape_squeeze.3
  12.6 0.3 fusion
  13.0 0.5 broadcast.212
  13.5 1.2 reduce.2
  14.6 0.0 copy-start.1
  14.7 1.6 reshape.98
  16.3 24.0 %all-to-all-start = ((bf16[64,2,3136]{2,1,0:T(2,128)(2,1)}), bf16[64,2,3136]{2,1,0:T(2,128)(2,1)}, u32[]{:S(2)}, u32[]{:S(2)}) async-start(bf16[64,2,3136]{2,1,0:T(2,128)(2,1)} %reshape.98), calls=%async_computation | async-start | bytes 1638400 | tf_op jit(solution)/shard_map/all_to_all | solution.py:64
  40.3 0.0 reduce-scatter.4.cloned.1.call-start
  40.4 0.0 copy-done.1
  40.4 0.1 select_reduce_fusion.1
  40.5 0.1 select_reduce_fusion
  40.7 20.8 %all-to-all-done = bf16[64,2,3136]{2,1,0:T(2,128)(2,1)} async-done(((bf16[64,2,3136]{2,1,0:T(2,128)(2,1)}), bf16[64,2,3136]{2,1,0:T(2,128)(2,1)}, u32[]{:S(2)}, u32[]{:S(2)}) %all-to-all-start) | async-done | bytes 802848 | tf_op jit(solution)/shard_map/all_to_all | solution.py:64
  61.5 5.4 %reshape.99 = bf16[64,1,6272]{2,1,0:T(2,128)(2,1)S(1)} reshape(bf16[64,2,3136]{2,1,0:T(2,128)(2,1)} %all-to-all-done) | data formatting | bytes 1605632
  66.9 0.2 convolution_convert_fusion.1
  67.1 0.9 reshape.88
  68.0 0.0 copy-done
  68.0 2.6 convolution_bitcast_fusion
  70.6 4.7 %copy.22 = f32[1728,392]{1,0:T(8,128)} copy(f32[1728,392]{0,1:T(8,128)} %convolution_bitcast_fusion) | data formatting | bytes 5419008 | tf_op jit(solution)/shard_map/dot_general | solution.py:82
  75.3 4.5 %reshape_reshape.3 = f32[2,8,4,27,392]{4,3,2,1,0:T(8,128)} reshape(f32[1728,392]{1,0:T(8,128)} %copy.22) | data formatting | bytes 5419008 | tf_op jit(solution)/shard_map/reshape;reshape | solution.py:13
  79.8 6.7 %copy.23 = f32[4,8,2,27,392]{4,2,1,0,3:T(2,128)} copy(f32[4,8,2,27,392]{4,3,0,1,2:T(8,128)} %bitcast.30) | data formatting | bytes 5419008 | tf_op jit(solution)/shard_map/transpose | solution.py:14
  86.5 5.5 %reshape.89 = f32[64,27,392]{2,0,1:T(8,128)} reshape(f32[4,8,2,27,392]{4,2,1,0,3:T(2,128)} %copy.23) | data formatting | bytes 5419008 | tf_op jit(solution)/shard_map/reshape | solution.py:14
  92.0 0.0 reduce-scatter.4.cloned.1.call-update
  92.0 0.0 all-reduce.5.cloned.1.call-start
  92.1 62.0 %reduce-scatter.4.cloned.1.call-done = f32[16,27,392]{2,0,1:T(8,128)} async-done(((f32[64,27,392]{2,0,1:T(8,128)}), f32[16,27,392]{2,0,1:T(8,128)}) %reduce-scatter.4.cloned.1.call-update) | async-done | bytes 677392 | tf_op jit(solution)/shard_map/reduce_scatter | solution.py:16
  154.0 0.0 all-reduce.5.cloned.1.call-update
  154.1 0.0 all-reduce.7.cloned.1.call-start
  154.1 1.3 dynamic-slice
  156.0 82.0 %all-reduce.5.cloned.1.call-done = f32[16,27,392]{2,0,1:T(8,128)} async-done(((f32[16,27,392]{2,0,1:T(8,128)}), f32[16,27,392]{2,0,1:T(8,128)}) %all-reduce.5.cloned.1.call-update) | async-done | bytes 677392
  238.1 1.7 constant_dynamic-slice_fusion.1
  239.8 0.0 all-reduce.7.cloned.1.call-update
  239.8 1.3 dynamic-slice.2
  241.1 57.2 %all-reduce.7.cloned.1.call-done = f32[2,27,392]{2,0,1:T(2,128)} async-done(((f32[2,27,392]{2,0,1:T(2,128)}), f32[2,27,392]{2,0,1:T(2,128)}) %all-reduce.7.cloned.1.call-update) | async-done | bytes 84688
  298.3 1.6 constant_dynamic-slice_fusion
  299.9 0.1 broadcast_in_dim.44
  300.0 32.3 %all_to_all.17 = f32[12,27,392]{2,1,0:T(8,128)S(1)} all-to-all(f32[12,27,392]{2,1,0:T(8,128)S(1)} %broadcast_in_dim.44), channel_id=1, replica_groups=mesh['dp'=12,'enc_0'=2,'enc_1'=8,'enc_2'=4] {'dp'}, dimensions={0} | all-to-all | bytes 1016064 | tf_op jit(solution)/shard_map/all_to_all | solution.py:32
  332.3 0.7 reduce_sum.49
  (4 shorter events, 0.0 us)
Async XLA Ops:
  6.5 61.5 %copy-start = (bf16[1,384,1728]{1,2,0:T(8,128)(2,1)S(1)}, bf16[1,384,1728]{1,2,0:T(8,128)(2,1)}, u32[]{:S(2)}) copy-start(bf16[1,384,1728]{1,2,0:T(8,128)(2,1)} %param.5) | copy-start | bytes 3981316
  14.6 25.7 %copy-start.1 = (s32[1,64]{1,0:T(1,128)S(1)}, s32[1,64]{1,0:T(1,128)}, u32[]{:S(2)}) copy-start(s32[1,64]{1,0:T(1,128)} %param.3) | copy-start | bytes 772
  16.3 45.2 %all-to-all-start = ((bf16[64,2,3136]{2,1,0:T(2,128)(2,1)}), bf16[64,2,3136]{2,1,0:T(2,128)(2,1)}, u32[]{:S(2)}, u32[]{:S(2)}) async-start(bf16[64,2,3136]{2,1,0:T(2,128)(2,1)} %reshape.98), calls=%async_computation | async-start | bytes 1638400 | tf_op jit(solution)/shard_map/all_to_all | solution.py:64
  40.3 113.7 %reduce-scatter.4.cloned.1.call-start = ((), (), s32[]{:S(2)}) async-start(), calls=%async_computation.3 | async-start | bytes 4423680 | tf_op jit(solution)/shard_map/reduce_scatter | solution.py:16
  92.0 146.1 %all-reduce.5.cloned.1.call-start = ((), (), s32[]{:S(2)}) async-start(), calls=%async_computation.4 | async-start | bytes 1769472
  154.1 144.2 %all-reduce.7.cloned.1.call-start = ((), (), s32[]{:S(2)}) async-start(), calls=%async_computation.5 | async-start | bytes 221184
Sparse Core Ops, SparseCore 0:
  92.1 61.8 reduce-scatter.3
  156.4 81.6 all-reduce.4
  241.2 56.9 all-reduce.6
where the time goes:
time: 340 us
  waiting for transfers between devices  222 us (65%)
  local copies, waits for them, and re-layouts  38.9 us (11%)
  blocking collectives  32.3 us (9%)
  starting transfers between devices  24.1 us (7%)
  between operations  13.9 us (4%)
  other arithmetic  5.03 us (1%)
    unnamed x5, waiting for transfers between devices  139 us
    reduce_scatter x1, waiting for transfers between devices, sum_in_order(): blocks = lax.psum_scatter(blocks, axes[k], scatter_dimension=0, tiled=True)  62 us
    all_to_all x1, blocking collectives, copy_for_each(): return lax.all_to_all(copies, axis, split_axis=0, concat_axis=0, tiled=True)  32.3 us
    all_to_all x1, starting transfers between devices, per_device(): lax.all_to_all(outgoing, ENC, split_axis=0, concat_axis=0, tiled=True)  24 us
    all_to_all x1, waiting for transfers between devices, per_device(): lax.all_to_all(outgoing, ENC, split_axis=0, concat_axis=0, tiled=True)  20.8 us
    unnamed x12, local copies, waits for them, and re-layouts  14.3 us
  transfers between devices with their start and end apart: 4, of which 4 were waited for; matrix products, arithmetic and copies ran while one was open for 1% of the time, Pallas kernels for 0%

commit v1 on v0

v1 whole, which is shorter than its diff:
```python
import functools

import jax
import jax.numpy as jnp
from jax import lax
from jax.experimental import pallas as pl
from jax.experimental.pallas import tpu as pltpu
from jax.sharding import Mesh
from jax.sharding import PartitionSpec as P

BLK = 16
LANES = 128
TILES = 3
REST = 8
MSG = TILES * BLK + REST
PART = 14
HALF = 44
ENC = ("zh", "y", "x")
Z = ("zh", "zl")


def pack_kernel(me_ref, counts_ref, pix_ref, out_ref, rows_ref):
    n_enc = counts_ref.shape[1]
    patches = pix_ref.shape[1]
    me = me_ref[0]
    start = lax.fori_loop(
        0, n_enc, lambda e, total: total + jnp.where(e < me, counts_ref[0, e], 0), 0
    )
    side = 256
    eye = (
        lax.broadcasted_iota(jnp.int32, (side, side), 0)
        == lax.broadcasted_iota(jnp.int32, (side, side), 1)
    ).astype(jnp.bfloat16)
    for b in range(patches // side):
        turned = lax.dot_general(
            eye,
            pix_ref[: TILES * LANES, b * side : (b + 1) * side],
            (((1,), (1,)), ((), ())),
            preferred_element_type=jnp.float32,
        )
        rows_ref[b * side : (b + 1) * side, :] = turned.astype(jnp.bfloat16)
    for s in range(patches // BLK):
        t = lax.rem(start + s, n_enc)
        for j in range(TILES):
            out_ref[t, j * BLK : (j + 1) * BLK, :] = rows_ref[
                s * BLK : (s + 1) * BLK, j * LANES : (j + 1) * LANES
            ]
        chunk = s * BLK // LANES
        out_ref[t, TILES * BLK :, :] = pix_ref[
            TILES * LANES :, chunk * LANES : (chunk + 1) * LANES
        ]


def grad_kernel(me_ref, counts_ref, arrived_ref, cot_ref, out_ref, rows_ref, rest_ref, sums_ref):
    n_enc = counts_ref.shape[1]
    depth = cot_ref.shape[1]
    me = me_ref[0]
    lane = lax.broadcasted_iota(jnp.int32, (REST, LANES), 1)
    per_tile = LANES // BLK

    def place(e, start):
        count = counts_ref[0, e]
        slot = lax.rem(me - lax.rem(start, n_enc) + n_enc, n_enc)

        @pl.when(slot < count)
        def _():
            k = (start + slot) // n_enc
            to = pl.ds(pl.multiple_of(k * BLK, BLK), BLK)
            for j in range(TILES):
                rows_ref[to, j * LANES : (j + 1) * LANES] = arrived_ref[
                    e, j * BLK : (j + 1) * BLK, :
                ]
            there, here = lax.rem(slot, per_tile), lax.rem(k, per_tile)
            moved = pltpu.roll(
                arrived_ref[e, TILES * BLK :, :].astype(jnp.float32),
                lax.rem(here - there + per_tile, per_tile) * BLK,
                1,
            )
            tile = k // per_tile
            rest_ref[tile] = jnp.where(lane // BLK == here, moved, rest_ref[tile])

        return start + count

    lax.fori_loop(0, n_enc, place, 0)
    rest = jnp.concatenate([rest_ref[i] for i in range(depth // LANES)], axis=1)
    spread = jnp.concatenate([rest] * (LANES // REST), axis=0).astype(jnp.bfloat16)
    step = cot_ref.shape[0] // 4

    def multiply(m, _):
        at = pl.ds(pl.multiple_of(m * step, 16), step)
        cot = cot_ref[at, :]
        sums_ref[at, : TILES * LANES] = jnp.dot(
            cot, rows_ref[...], preferred_element_type=jnp.float32
        )
        sums_ref[at, TILES * LANES :] = lax.dot_general(
            cot, spread, (((1,), (1,)), ((), ())), preferred_element_type=jnp.float32
        )
        return 0

    lax.fori_loop(0, 4, multiply, 0)

    _, nx, ny, _, _ = out_ref.shape
    own = cot_ref.shape[0] // n_enc
    mine = (
        lax.broadcasted_iota(jnp.int32, (PART, LANES), 1) // REST
        == lax.broadcasted_iota(jnp.int32, (PART, LANES), 0)
    )

    def pack(pair, _):
        base = pl.multiple_of(pair * (2 * nx * own), 8)
        for zh in range(2):
            for b in range(2 * nx):
                y, x = pair * 2 + b // nx, b % nx
                for c in range(2):
                    first = zh * nx * ny * own + b * own + c * (own - PART)
                    low = first // 8 * 8
                    span = pl.cdiv(first - low + PART, 8) * 8
                    part = sums_ref[pl.ds(pl.multiple_of(base + low, 8), span), :][
                        first - low : first - low + PART
                    ]
                    for j in range(TILES):
                        out_ref[c, x, y, zh * HALF + j * PART : zh * HALF + (j + 1) * PART, :] = (
                            part[:, j * LANES : (j + 1) * LANES]
                        )
                    rest_row = jnp.sum(
                        jnp.where(mine, part[:, TILES * LANES :], 0.0), axis=0, keepdims=True
                    )
                    out_ref[c, x, y, zh * HALF + TILES * PART : (zh + 1) * HALF, :] = (
                        jnp.broadcast_to(rest_row, (HALF - TILES * PART, LANES))
                    )
        return 0

    lax.fori_loop(0, ny // 2, pack, 0)


def unpack_kernel(parts_ref, out_ref):
    own = out_ref.shape[0]
    for c in range(2):
        first, skip = (0, 0) if c == 0 else (PART, 2 * PART - own)
        for j in range(TILES):
            out_ref[first : first + PART - skip, j * LANES : (j + 1) * LANES] = parts_ref[
                c, j * PART + skip : (j + 1) * PART, :
            ]
        row = parts_ref[c, TILES * PART : TILES * PART + 1, :]
        for r in range(skip, PART):
            out_ref[first + r - skip : first + r - skip + 1, TILES * LANES :] = row[
                :, r * REST : (r + 1) * REST
            ]


def exchange(value, axes):
    return lax.all_to_all(value, axes, split_axis=0, concat_axis=0, tiled=True)


def per_device(counts, pixels, cotangent):
    n_enc = lax.axis_size(ENC)
    nx, ny, nzl = lax.axis_size("x"), lax.axis_size("y"), lax.axis_size("zl")
    me = lax.axis_index(ENC).astype(jnp.int32)[None]
    vmem = pl.BlockSpec(memory_space=pltpu.VMEM)
    smem = pl.BlockSpec(memory_space=pltpu.SMEM)
    pix = pixels[0].T
    cot = cotangent[0].T
    width, depth = cot.shape
    messages = pl.pallas_call(
        pack_kernel,
        out_shape=jax.ShapeDtypeStruct((n_enc, MSG, LANES), jnp.bfloat16),
        in_specs=[smem, smem, vmem],
        out_specs=vmem,
        scratch_shapes=[pltpu.VMEM((pix.shape[1], TILES * LANES), jnp.bfloat16)],
    )(me, counts, pix)
    arrived = exchange(messages, ENC)
    terms = pl.pallas_call(
        grad_kernel,
        out_shape=jax.ShapeDtypeStruct((2, nx, ny, 2 * HALF, LANES), jnp.float32),
        in_specs=[smem, smem, vmem, vmem],
        out_specs=vmem,
        scratch_shapes=[
            pltpu.VMEM((depth, TILES * LANES), jnp.bfloat16),
            pltpu.VMEM((depth // LANES, REST, LANES), jnp.float32),
            pltpu.VMEM((width, (TILES + 1) * LANES), jnp.float32),
        ],
    )(me, counts, arrived, cot)
    terms = jnp.sum(exchange(terms.reshape(2, -1, LANES), "core").reshape(terms.shape), axis=0)
    terms = jnp.sum(exchange(terms.reshape(nx, -1, LANES), "x"), axis=0)
    terms = jnp.sum(exchange(terms.reshape(ny, -1, LANES), "y"), axis=0)
    terms = terms.reshape(2, 1, HALF, LANES)
    terms = jnp.broadcast_to(terms, (2, nzl, HALF, LANES)).reshape(2 * nzl, HALF, LANES)
    terms = jnp.sum(exchange(terms, Z), axis=0)
    parts = exchange(jnp.broadcast_to(terms, (2, HALF, LANES)), "core")
    return pl.pallas_call(
        unpack_kernel,
        out_shape=jax.ShapeDtypeStruct((width // n_enc, pix.shape[0]), jnp.float32),
        in_specs=[vmem],
        out_specs=vmem,
    )(parts)


def solution(mesh):
    torus = Mesh(mesh.devices.reshape(6, 2, 2, 8, 4), ("zl", "core", "zh", "y", "x"))
    dp = ("zl", "core")
    return jax.shard_map(
        per_device,
        mesh=torus,
        in_specs=(P(dp, None), P(dp, ENC, None), P(dp, ENC, None)),
        out_specs=P(ENC, None),
        check_vma=False,
    )
```

time: 340 us -> 156 us (0.46)
  waiting for transfers between devices: 222 us -> 0 us
  blocking collectives: 32.3 us -> 142 us
  local copies, waits for them, and re-layouts: 38.9 us -> 0.03 us
  starting transfers between devices: 24.1 us -> 0 us
  between operations: 13.9 us -> 0.04 us
  Pallas kernels: 0 us -> 11.9 us
  other arithmetic: 5.03 us -> 1.59 us
    unnamed x5 -> x0, waiting for transfers between devices: 139 us -> none
    all_to_all x1 -> x6, blocking collectives: 32.3 us -> 142 us  [exchange(): return lax.all_to_all(value, axes, split_axis=0, concat_axis=0, tiled=True)]
    reduce_scatter x1 -> x0, waiting for transfers between devices: 62 us -> none  [sum_in_order(): blocks = lax.psum_scatter(blocks, axes[k], scatter_dimension=0, tiled=True)]
    all_to_all x1 -> x0, starting transfers between devices: 24 us -> none  [per_device(): lax.all_to_all(outgoing, ENC, split_axis=0, concat_axis=0, tiled=True)]
    all_to_all x1 -> x0, waiting for transfers between devices: 20.8 us -> none  [per_device(): lax.all_to_all(outgoing, ENC, split_axis=0, concat_axis=0, tiled=True)]
    unnamed x12 -> x0, local copies, waits for them, and re-layouts: 14.3 us -> none
    pallas_call x0 -> x3, Pallas kernels: none -> 11.9 us  [the longest x1 7.56 us: per_device(): pl.pallas_call(grad_kernel, out_shape=jax.ShapeDtypeStruct((2, nx, ny, 2...]
    reshape x3 -> x0, local copies, waits for them, and re-layouts: 7.2 us -> none  [the longest x1 5.46 us: sum_in_order(): blocks = jnp.moveaxis(blocks, turns, range(len(axes))).reshape(-1, *inside)]
  transfers between devices with their start and end apart: 4 -> 0, of which waited for: 4 -> 0; matrix products, arithmetic and copies ran while one was open for 1% -> 0% of each run, Pallas kernels for 0% -> 0%
where the time goes in v1:
time: 156 us; the launch traced here: 155 us
  blocking collectives  142 us (91%)
  Pallas kernels  11.9 us (8%)
  other arithmetic  1.59 us (1%)
    all_to_all x6, blocking collectives, exchange(): return lax.all_to_all(value, axes, split_axis=0, concat_axis=0, tiled=True)  142 us
    pallas_call x1, Pallas kernels, per_device(): pl.pallas_call(grad_kernel, out_shape=jax.ShapeDtypeStruct((2, nx, ny, 2...  7.56 us

profile of v1, /device:TPU:1, one launch (start us, length us, event | category | flops | bytes accessed | tf_op | source)
XLA Modules:
  0.0 155.4 jit_solution(6144688740444457036)
XLA Ops:
  0.0 2.8 %shard_map.37 = bf16[64,56,128]{2,1,0:T(8,128)(2,1)} custom-call(s32[1]{0:T(128)} %bitcast.me_ref, s32[1,64]{1,0:T(1,128)} %counts_ref.3, bf16[392,768]{1,0:T(8,128)(2,1)} %bitcast.16), custom_call_target="tpu_custom_call" | custom-call | tf_op jit(solution)/shard_map/pallas_call | solution.py:164
  2.8 46.7 %all_to_all.30.arrived_ref = bf16[64,56,128]{2,1,0:T(8,128)(2,1)} all-to-all(bf16[64,56,128]{2,1,0:T(8,128)(2,1)} %shard_map.37), channel_id=1, replica_groups=mesh['zl'=6,'core'=2,'zh'=2,'y'=8,'x'=4] {'zh','y','x'}, dimensions={0} | all-to-all | bytes 1835008 | tf_op jit(solution)/shard_map/all_to_all | solution.py:152
  49.5 7.6 %shard_map.38 = f32[2,4,8,88,128]{4,3,2,1,0:T(8,128)} custom-call(s32[1]{0:T(128)} %bitcast.me_ref, s32[1,64]{1,0:T(1,128)} %counts_ref.3, bf16[64,56,128]{2,1,0:T(8,128)(2,1)} %all_to_all.30.arrived_ref, bf16[1728,384]{1,0:T(8,128)(2,1)} %bitcast.14), custom_call_target="tpu_custom_call" | custom-call | tf_op jit(solution)/shard_map/pallas_call | solution.py:172
  57.1 9.1 %all_to_all.31 = f32[2,2816,128]{2,1,0:T(8,128)S(1)} all-to-all(f32[2,2816,128]{2,1,0:T(8,128)} %bitcast.11), channel_id=1, replica_groups=mesh['zl'=6,'core'=2,'zh'=2,'y'=8,'x'=4] {'core'}, dimensions={0} | all-to-all | bytes 5767168 | tf_op jit(solution)/shard_map/all_to_all | solution.py:152
  66.2 1.4 reduce_sum.36
  67.6 22.5 %all_to_all.32 = f32[4,704,128]{2,1,0:T(8,128)S(1)} all-to-all(f32[4,704,128]{2,1,0:T(8,128)} %bitcast.12), channel_id=1, replica_groups=mesh['zl'=6,'core'=2,'zh'=2,'y'=8,'x'=4] {'x'}, dimensions={0} | all-to-all | bytes 2883584 | tf_op jit(solution)/shard_map/all_to_all | solution.py:152
  90.1 0.1 reduce_sum.37
  90.2 17.4 %all_to_all.33 = f32[8,88,128]{2,1,0:T(8,128)S(1)} all-to-all(f32[8,88,128]{2,1,0:T(8,128)S(1)} %bitcast.13), channel_id=1, replica_groups=mesh['zl'=6,'core'=2,'zh'=2,'y'=8,'x'=4] {'y'}, dimensions={0} | all-to-all | bytes 720896 | tf_op jit(solution)/shard_map/all_to_all | solution.py:152
  107.6 37.3 %all_to_all.34 = f32[12,44,128]{2,1,0:T(8,128)S(1)} all-to-all(f32[12,44,128]{2,1,0:T(8,128)S(1)} %bitcast.15), channel_id=1, replica_groups=mesh['zl'=6,'core'=2,'zh'=2,'y'=8,'x'=4] {'zh','zl'}, dimensions={0} | all-to-all | bytes 540672 | tf_op jit(solution)/shard_map/all_to_all | solution.py:152
  144.9 8.9 %all_to_all.35.parts_ref = f32[2,44,128]{2,1,0:T(8,128)} all-to-all(f32[2,44,128]{2,1,0:T(8,128)S(1)} %broadcast_in_dim.16), channel_id=1, replica_groups=mesh['zl'=6,'core'=2,'zh'=2,'y'=8,'x'=4] {'core'}, dimensions={0} | all-to-all | bytes 90112 | tf_op jit(solution)/shard_map/all_to_all | solution.py:152
  153.9 1.5 shard_map.39
  (5 shorter events, 0.1 us)

commit v2 on v1

v2 whole, which is shorter than its diff:
```python
import jax
import jax.numpy as jnp
from jax import lax
from jax.experimental import pallas as pl
from jax.experimental.pallas import tpu as pltpu
from jax.sharding import Mesh
from jax.sharding import PartitionSpec as P


BLK = 16
LANES = 128
TILES = 3
REST = 8
MSG = TILES * BLK + REST
PART = 16
HALF = TILES * PART
ENC = ("zh", "y", "x")
Z = ("zh", "zl")
MIB = 1024 * 1024


def pack_kernel(at_ref, counts_ref, pix_ref, out_ref, rows_ref):
    n_enc = counts_ref.shape[1]
    whole, patches = rows_ref.shape[1], pix_ref.shape[1]
    me = at_ref[0]
    start = lax.fori_loop(
        0, n_enc, lambda e, total: total + jnp.where(e < me, counts_ref[0, e], 0), 0
    )
    side = 256
    eye = (
        lax.broadcasted_iota(jnp.int32, (side, side), 0)
        == lax.broadcasted_iota(jnp.int32, (side, side), 1)
    ).astype(jnp.bfloat16)
    for b in range(patches // side):
        turned = lax.dot_general(
            eye,
            pix_ref[:whole, b * side : (b + 1) * side],
            (((1,), (1,)), ((), ())),
            preferred_element_type=jnp.float32,
        )
        rows_ref[b * side : (b + 1) * side, :] = turned.astype(jnp.bfloat16)
    for s in range(patches // BLK):
        t = lax.rem(start + s, n_enc)
        for j in range(TILES):
            out_ref[t, j * BLK : (j + 1) * BLK, :] = rows_ref[
                s * BLK : (s + 1) * BLK, j * LANES : (j + 1) * LANES
            ]
        chunk = s * BLK // LANES
        out_ref[t, TILES * BLK :, :] = pix_ref[whole:, chunk * LANES : (chunk + 1) * LANES]


def cut_kernel(at_ref, cot_ref, *refs):
    *out_refs, wide_ref, cut_ref = refs
    nx, _, rows, _ = cut_ref.shape
    shards = rows // PART
    own = cot_ref.shape[0] // (nx * shards)
    step = cot_ref.shape[0] // 4
    for m in range(4):
        at = slice(m * step, (m + 1) * step)
        wide_ref[at, :] = cot_ref[at, :].astype(jnp.float32)

    def cut(pair, _):
        base = pl.multiple_of(pair * (2 * nx * own), 8)
        for zh in range(2):
            for b in range(2 * nx):
                to = pl.multiple_of(pair * (4 * PART), PART) + (b // nx * 2 + zh) * PART
                for c in range(2):
                    first = zh * nx * (shards // 2) * own + b * own + c * (own - PART)
                    low = first // 8 * 8
                    span = pl.cdiv(first - low + PART, 8) * 8
                    part = wide_ref[pl.ds(pl.multiple_of(base + low, 8), span), :][
                        first - low : first - low + PART
                    ]
                    cut_ref[b % nx, c, pl.ds(pl.multiple_of(to, PART), PART), :] = part.astype(
                        jnp.bfloat16
                    )
        return 0

    lax.fori_loop(0, shards // 4, cut, 0)
    for d, out_ref in enumerate(out_refs):
        out_ref[...] = cut_ref[lax.rem(at_ref[2] + d, nx)]


def place_kernel(at_ref, counts_ref, arrived_ref, out_ref, rest_ref):
    n_enc = counts_ref.shape[1]
    depth = out_ref.shape[1]
    me = at_ref[0]
    lane = lax.broadcasted_iota(jnp.int32, (REST, LANES), 1)
    per_tile = LANES // BLK

    def place(e, start):
        count = counts_ref[0, e]
        slot = lax.rem(me - lax.rem(start, n_enc) + n_enc, n_enc)

        @pl.when(slot < count)
        def _():
            k = (start + slot) // n_enc
            to = pl.ds(pl.multiple_of(k * BLK, BLK), BLK)
            for j in range(TILES):
                out_ref[to, j * LANES : (j + 1) * LANES] = arrived_ref[
                    e, j * BLK : (j + 1) * BLK, :
                ]
            there, here = lax.rem(slot, per_tile), lax.rem(k, per_tile)
            moved = pltpu.roll(
                arrived_ref[e, TILES * BLK :, :].astype(jnp.float32),
                lax.rem(here - there + per_tile, per_tile) * BLK,
                1,
            )
            tile = k // per_tile
            rest_ref[tile] = jnp.where(lane // BLK == here, moved, rest_ref[tile])

        return start + count

    lax.fori_loop(0, n_enc, place, 0)
    rest = jnp.concatenate([rest_ref[i] for i in range(depth // LANES)], axis=1)
    out_ref[depth:, :] = jnp.concatenate([rest, rest], axis=0).astype(jnp.bfloat16)


def grad_kernel(at_ref, *refs):
    keep_ref, send_ref, sums_ref = refs[-3:]
    nx = (len(refs) - 3) // 2
    cut_refs, pix_refs = refs[:nx], refs[nx : 2 * nx]
    rows, depth = cut_refs[0].shape[1:]
    for c in range(2):
        whole = rest = 0.0
        for cut_ref, pix_ref in zip(cut_refs, pix_refs):
            cut = cut_ref[c]
            whole += jnp.dot(cut, pix_ref[:depth, :], preferred_element_type=jnp.float32)
            spread = jnp.concatenate([pix_ref[depth:, :]] * (LANES // (2 * REST)), axis=0)
            rest += lax.dot_general(
                cut, spread, (((1,), (1,)), ((), ())), preferred_element_type=jnp.float32
            )
        sums_ref[c, :, : TILES * LANES] = whole
        sums_ref[c, :, TILES * LANES :] = rest
    place = lax.broadcasted_iota(jnp.int32, (PART, LANES), 0)
    mine = lax.broadcasted_iota(jnp.int32, (PART, LANES), 1) // REST == place
    for out_ref, c in ((keep_ref, at_ref[1]), (send_ref, 1 - at_ref[1])):
        spare = jnp.where(c == 0, PART - 1, 0)
        for q in range(rows // PART):
            y, zh = q // 2, q % 2
            at = slice(q * PART, (q + 1) * PART)
            row = jnp.sum(
                jnp.where(mine, sums_ref[c, at, TILES * LANES :], 0.0), axis=0, keepdims=True
            )
            for j in range(TILES):
                tile = sums_ref[c, at, j * LANES : (j + 1) * LANES]
                if j == 0:
                    tile = jnp.where(place == spare, row, tile)
                out_ref[y, zh * HALF + j * PART : zh * HALF + (j + 1) * PART, :] = tile


def fan_kernel(term_ref, out_ref):
    nz = out_ref.shape[0]
    total = jnp.sum(term_ref[...], axis=0)
    for z in range(nz):
        zh = z // (nz // 2)
        out_ref[z] = total[zh * HALF : (zh + 1) * HALF]


def unpack_kernel(parts_ref, out_ref):
    own = out_ref.shape[0]
    cut = own // 2 + 1
    for c, low, high, first in ((0, 0, cut, 0), (1, cut, own, own - PART)):
        for j in range(TILES):
            out_ref[low:high, j * LANES : (j + 1) * LANES] = parts_ref[
                c, j * PART + low - first : j * PART + high - first, :
            ]
        spare = PART - 1 if c == 0 else 0
        row = parts_ref[c, spare : spare + 1, :]
        for r in range(low, high):
            out_ref[r : r + 1, TILES * LANES :] = row[:, (r - first) * REST : (r - first + 1) * REST]


def exchange(value, axes):
    return lax.all_to_all(value, axes, split_axis=0, concat_axis=0, tiled=True)


def shift(value, axis, by):
    size = lax.axis_size(axis)
    return lax.ppermute(value, axis, [(i, (i + by) % size) for i in range(size)])


def call(kernel, out_shape, scratch, args, scalars, mib):
    spaces = [pltpu.SMEM] * scalars + [pltpu.VMEM] * (len(args) - scalars)
    return pl.pallas_call(
        kernel,
        out_shape=out_shape,
        in_specs=[pl.BlockSpec(memory_space=space) for space in spaces],
        out_specs=jax.tree.map(lambda _: pl.BlockSpec(memory_space=pltpu.VMEM), out_shape),
        scratch_shapes=scratch,
        compiler_params=pltpu.CompilerParams(vmem_limit_bytes=mib * MIB),
        cost_estimate=pl.CostEstimate(flops=0, bytes_accessed=6 * MIB, transcendentals=0),
    )(*args)


def gradient(counts, pixels, cotangent):
    n_enc = lax.axis_size(ENC)
    nx, ny, nzl = lax.axis_size("x"), lax.axis_size("y"), lax.axis_size("zl")
    at = jnp.stack([lax.axis_index(ENC), lax.axis_index("core"), lax.axis_index("x")])
    at = at.astype(jnp.int32)
    pix, cot = pixels[0].T, cotangent[0].T
    width, depth = cot.shape
    bf16 = lambda *shape: jax.ShapeDtypeStruct(shape, jnp.bfloat16)
    f32 = lambda *shape: jax.ShapeDtypeStruct(shape, jnp.float32)
    rows = 2 * ny * PART

    messages = call(
        pack_kernel,
        bf16(n_enc, MSG, LANES),
        [pltpu.VMEM((pix.shape[1], TILES * LANES), jnp.bfloat16)],
        (at, counts, pix),
        2,
        8,
    )
    arrived = exchange(messages, ENC)
    cuts = call(
        cut_kernel,
        [bf16(2, rows, depth)] * nx,
        [pltpu.VMEM((width, depth), jnp.float32), pltpu.VMEM((nx, 2, rows, depth), jnp.bfloat16)],
        (at, cot),
        1,
        12,
    )
    cuts = [cuts[0]] + [shift(cuts[d], "x", d) for d in range(1, nx)]
    placed = call(
        place_kernel,
        bf16(depth + 2 * REST, TILES * LANES),
        [pltpu.VMEM((depth // LANES, REST, LANES), jnp.float32)],
        (at, counts, arrived),
        2,
        8,
    )
    row = [placed] + [shift(placed, "x", d) for d in range(1, nx)]
    keep, send = call(
        grad_kernel,
        [f32(ny, 2 * HALF, LANES)] * 2,
        [pltpu.VMEM((2, rows, (TILES + 1) * LANES), jnp.float32)],
        (at, *cuts, *row),
        1,
        16,
    )
    terms = keep + shift(send, "core", 1)
    terms = exchange(terms, "y")
    terms = call(fan_kernel, f32(2 * nzl, HALF, LANES), [], (terms,), 0, 8)
    terms = jnp.sum(exchange(terms, Z), axis=0)
    parts = exchange(jnp.broadcast_to(terms, (2, HALF, LANES)), "core")
    return call(unpack_kernel, f32(width // n_enc, pix.shape[0]), [], (parts,), 0, 8)


def solution(mesh):
    torus = Mesh(mesh.devices.reshape(6, 2, 2, 8, 4), ("zl", "core", "zh", "y", "x"))
    dp = ("zl", "core")
    return jax.shard_map(
        gradient,
        mesh=torus,
        in_specs=(P(dp, None), P(dp, ENC, None), P(dp, ENC, None)),
        out_specs=P(ENC, None),
        check_vma=False,
    )
```

time: 156 us -> 148 us (0.949)
  blocking collectives: 142 us -> 64.3 us
  starting transfers between devices: 0 us -> 46 us
  waiting for transfers between devices: 0 us -> 25.6 us
  Pallas kernels: 11.9 us -> 9.95 us
  local copies, waits for them, and re-layouts: 0.03 us -> 1.74 us
    all_to_all x6 -> x3, blocking collectives: 142 us -> 64.3 us  [exchange(): return lax.all_to_all(value, axes, split_axis=0, concat_axis=0, tiled=True)]
    all_to_all x0 -> x1, starting transfers between devices: none -> 23.9 us  [exchange(): return lax.all_to_all(value, axes, split_axis=0, concat_axis=0, tiled=True)]
    ppermute x0 -> x7, starting transfers between devices: none -> 22.1 us  [shift(): lax.ppermute(value, axis, [(i, (i + by) % size) for i in range(size)])]
    ppermute x0 -> x7, waiting for transfers between devices: none -> 15.5 us  [shift(): lax.ppermute(value, axis, [(i, (i + by) % size) for i in range(size)])]
    all_to_all x0 -> x1, waiting for transfers between devices: none -> 10.2 us  [exchange(): return lax.all_to_all(value, axes, split_axis=0, concat_axis=0, tiled=True)]
    pallas_call x3 -> x6, Pallas kernels: 11.9 us -> 9.95 us  [call(): pl.pallas_call(kernel, out_shape=out_shape, in_specs=[pl.BlockSpec(memory...]
    unnamed x0 -> x8, local copies, waits for them, and re-layouts: none -> 1.73 us
    reduce_sum x4 -> x1, other arithmetic: 1.59 us -> 0.02 us  [gradient(): terms = jnp.sum(exchange(terms, Z), axis=0)]
  transfers between devices with their start and end apart: 0 -> 8, of which waited for: 0 -> 4; matrix products, arithmetic and copies ran while one was open for 0% -> 0% of each run, Pallas kernels for 0% -> 3%
where the time goes in v2:
time: 148 us
  blocking collectives  64.3 us (43%)
  starting transfers between devices  46 us (31%)
  waiting for transfers between devices  25.6 us (17%)
  Pallas kernels  9.95 us (7%)
  local copies, waits for them, and re-layouts  1.74 us (1%)
    all_to_all x3, blocking collectives, exchange(): return lax.all_to_all(value, axes, split_axis=0, concat_axis=0, tiled=True)  64.3 us
    all_to_all x1, starting transfers between devices, exchange(): return lax.all_to_all(value, axes, split_axis=0, concat_axis=0, tiled=True)  23.9 us
    ppermute x7, starting transfers between devices, shift(): lax.ppermute(value, axis, [(i, (i + by) % size) for i in range(size)])  22.1 us
    ppermute x7, waiting for transfers between devices, shift(): lax.ppermute(value, axis, [(i, (i + by) % size) for i in range(size)])  15.5 us
    all_to_all x1, waiting for transfers between devices, exchange(): return lax.all_to_all(value, axes, split_axis=0, concat_axis=0, tiled=True)  10.2 us
    pallas_call x6, Pallas kernels, call(): pl.pallas_call(kernel, out_shape=out_shape, in_specs=[pl.BlockSpec(memory...  9.95 us
  transfers between devices with their start and end apart: 8, of which 4 were waited for; matrix products, arithmetic and copies ran while one was open for 0% of the time, Pallas kernels for 3%

profile of v2, /device:TPU:1, one launch (start us, length us, event | category | flops | bytes accessed | tf_op | source)
XLA Modules:
  0.0 147.9 jit_solution(5124153446131200301)
XLA Ops:
  0.0 0.1 pad_add_fusion.at_ref
  0.1 0.0 copy-start.1
  0.1 1.1 copy-done.1
  1.1 0.0 copy-start.2
  1.1 0.7 copy-done.2
  1.8 0.0 copy-start
  1.8 2.4 %shard_map.38 = bf16[64,56,128]{2,1,0:T(8,128)(2,1)} custom-call(s32[3]{0:T(128)S(1)} %pad_add_fusion.at_ref, s32[1,64]{1,0:T(1,128)S(1)} %copy-done.2, bf16[392,768]{1,0:T(8,128)(2,1)S(1)} %bitcast.10), custom_call_target="tpu_custom_call" | custom-call | bytes 6291456 | tf_op jit(solution)/shard_map/pallas_call | solution.py:185
  4.2 0.0 copy-start.3
  4.2 23.9 %all-to-all-start = ((bf16[64,56,128]{2,1,0:T(8,128)(2,1)}), bf16[64,56,128]{2,1,0:T(8,128)(2,1)S(1)}, u32[]{:S(2)}, u32[]{:S(2)}) async-start(bf16[64,56,128]{2,1,0:T(8,128)(2,1)} %shard_map.38), calls=%async_computation | async-start | bytes 1835008 | tf_op jit(solution)/shard_map/all_to_all | solution.py:175
  28.1 0.0 copy-done
  28.1 2.3 %shard_map.37 = (bf16[2,256,384]{2,1,0:T(8,128)(2,1)S(1)}, bf16[2,256,384]{2,1,0:T(8,128)(2,1)}, bf16[2,256,384]{2,1,0:T(8,128)(2,1)S(1)}, bf16[2,256,384]{2,1,0:T(8,128)(2,1)S(1)}) custom-call(s32[3]{0:T(128)S(1)} %pad_add_fusion.at_ref, bf16[1728,384]{1,0:T(8,128)(2,1)S(1)} %bitcast.9), custom_call_target="tpu_custom_call" | custom-call | bytes 6291456 | tf_op jit(solution)/shard_map/pallas_call | solution.py:185
  30.4 2.9 %collective-permute-start = (bf16[2,256,384]{2,1,0:T(8,128)(2,1)}, bf16[2,256,384]{2,1,0:T(8,128)(2,1)S(1)}, u32[]{:S(2)}, u32[]{:S(2)}) collective-permute-start(bf16[2,256,384]{2,1,0:T(8,128)(2,1)} %get-tuple-element.12), channel_id=1, source_target_pairs={{0,1},{1,2},{2,3},{3,0},{4,5},{5,6},{6,7},{7,4},{8,9},{9,10},{10,1... | collective-permute-start | bytes 1179656 | tf_op jit(solution)/shard_map/ppermute | solution.py:180
  33.3 4.3 %collective-permute-start.1 = (bf16[2,256,384]{2,1,0:T(8,128)(2,1)S(1)}, bf16[2,256,384]{2,1,0:T(8,128)(2,1)S(1)}, u32[]{:S(2)}, u32[]{:S(2)}) collective-permute-start(bf16[2,256,384]{2,1,0:T(8,128)(2,1)S(1)} %get-tuple-element.13), channel_id=1, source_target_pairs={{0,2},{1,3},{2,0},{3,1},{4,6},{5,7},{6,4},{7,5},{8,10},{9,11},{10,... | collective-permute-start | bytes 1179656 | tf_op jit(solution)/shard_map/ppermute | solution.py:180
  37.6 3.1 %collective-permute-start.2 = (bf16[2,256,384]{2,1,0:T(8,128)(2,1)S(1)}, bf16[2,256,384]{2,1,0:T(8,128)(2,1)S(1)}, u32[]{:S(2)}, u32[]{:S(2)}) collective-permute-start(bf16[2,256,384]{2,1,0:T(8,128)(2,1)S(1)} %get-tuple-element.14), channel_id=1, source_target_pairs={{0,3},{1,0},{2,1},{3,2},{4,7},{5,4},{6,5},{7,6},{8,11},{9,8},{10,9... | collective-permute-start | bytes 1179656 | tf_op jit(solution)/shard_map/ppermute | solution.py:180
  40.7 10.2 %all-to-all-done.arrived_ref = bf16[64,56,128]{2,1,0:T(8,128)(2,1)S(1)} async-done(((bf16[64,56,128]{2,1,0:T(8,128)(2,1)}), bf16[64,56,128]{2,1,0:T(8,128)(2,1)S(1)}, u32[]{:S(2)}, u32[]{:S(2)}) %all-to-all-start) | async-done | bytes 917536 | tf_op jit(solution)/shard_map/all_to_all | solution.py:175
  50.9 0.0 copy-done.3
  50.9 2.4 %shard_map.39.refs_4_ = bf16[400,384]{1,0:T(8,128)(2,1)S(1)} custom-call(s32[3]{0:T(128)S(1)} %pad_add_fusion.at_ref, s32[1,64]{1,0:T(1,128)S(1)} %copy-done.3, bf16[64,56,128]{2,1,0:T(8,128)(2,1)S(1)} %all-to-all-done.arrived_ref), custom_call_target="tpu_custom_call" | custom-call | bytes 6291456 | tf_op jit(solution)/shard_map/pallas_call | solution.py:185
  53.3 4.4 %collective-permute-start.5 = (bf16[400,384]{1,0:T(8,128)(2,1)S(1)}, bf16[400,384]{1,0:T(8,128)(2,1)S(1)}, u32[]{:S(2)}, u32[]{:S(2)}) collective-permute-start(bf16[400,384]{1,0:T(8,128)(2,1)S(1)} %shard_map.39.refs_4_), channel_id=1, source_target_pairs={{0,3},{1,0},{2,1},{3,2},{4,7},{5,4},{6,5},{7,6},{8,11},{9,8},{10,9... | collective-permute-start | bytes 921608 | tf_op jit(solution)/shard_map/ppermute | solution.py:180
  57.7 1.9 %collective-permute-start.4 = (bf16[400,384]{1,0:T(8,128)(2,1)S(1)}, bf16[400,384]{1,0:T(8,128)(2,1)S(1)}, u32[]{:S(2)}, u32[]{:S(2)}) collective-permute-start(bf16[400,384]{1,0:T(8,128)(2,1)S(1)} %shard_map.39.refs_4_), channel_id=1, source_target_pairs={{0,2},{1,3},{2,0},{3,1},{4,6},{5,7},{6,4},{7,5},{8,10},{9,11},{10,... | collective-permute-start | bytes 921608 | tf_op jit(solution)/shard_map/ppermute | solution.py:180
  59.6 0.0 collective-permute-done.refs_1_
  59.6 2.5 %collective-permute-start.3 = (bf16[400,384]{1,0:T(8,128)(2,1)S(1)}, bf16[400,384]{1,0:T(8,128)(2,1)S(1)}, u32[]{:S(2)}, u32[]{:S(2)}) collective-permute-start(bf16[400,384]{1,0:T(8,128)(2,1)S(1)} %shard_map.39.refs_4_), channel_id=1, source_target_pairs={{0,1},{1,2},{2,3},{3,0},{4,5},{5,6},{6,7},{7,4},{8,9},{9,10},{10,1... | collective-permute-start | bytes 921608 | tf_op jit(solution)/shard_map/ppermute | solution.py:180
  62.1 0.0 collective-permute-done.1.refs_2_
  62.1 0.0 collective-permute-done.2.refs_3_
  62.1 5.5 %collective-permute-done.5.refs_7_ = bf16[400,384]{1,0:T(8,128)(2,1)S(1)} collective-permute-done((bf16[400,384]{1,0:T(8,128)(2,1)S(1)}, bf16[400,384]{1,0:T(8,128)(2,1)S(1)}, u32[]{:S(2)}, u32[]{:S(2)}) %collective-permute-start.5) | collective-permute-done | bytes 307232 | tf_op jit(solution)/shard_map/ppermute | solution.py:180
  67.6 0.0 collective-permute-done.4.refs_6_
  67.6 8.6 %collective-permute-done.3.refs_5_ = bf16[400,384]{1,0:T(8,128)(2,1)S(1)} collective-permute-done((bf16[400,384]{1,0:T(8,128)(2,1)S(1)}, bf16[400,384]{1,0:T(8,128)(2,1)S(1)}, u32[]{:S(2)}, u32[]{:S(2)}) %collective-permute-start.3) | collective-permute-done | bytes 307232 | tf_op jit(solution)/shard_map/ppermute | solution.py:180
  76.2 2.2 %shard_map.40 = (f32[8,96,128]{2,1,0:T(8,128)S(1)}, f32[8,96,128]{2,1,0:T(8,128)S(1)}) custom-call(s32[3]{0:T(128)S(1)} %pad_add_fusion.at_ref, bf16[2,256,384]{2,1,0:T(8,128)(2,1)S(1)} %get-tuple-element.11.refs_0_, bf16[2,256,384]{2,1,0:T(8,128)(2,1)S(1)} %collective-permute-done.refs_1_, bf16[2,256,384]{2,1,0:T(8,128)(2,1)S(1)} %collective-permute-done.1.refs_2_, ...), custom_call_target="tpu_custom_call" | custom-call | bytes 6291456 | tf_op jit(solution)/shard_map/pallas_call | solution.py:185
  78.4 3.0 %collective-permute-start.6 = (f32[8,96,128]{2,1,0:T(8,128)S(1)}, f32[8,96,128]{2,1,0:T(8,128)S(1)}, u32[]{:S(2)}, u32[]{:S(2)}) collective-permute-start(f32[8,96,128]{2,1,0:T(8,128)S(1)} %get-tuple-element.16), channel_id=1, source_target_pairs={{0,64},{64,0},{1,65},{65,1},{2,66},{66,2},{3,67},{67,3},{4,68},{68... | collective-permute-start | bytes 1179656 | tf_op jit(solution)/shard_map/ppermute | solution.py:180
  81.4 1.3 collective-permute-done.6
  82.8 18.2 %all_to_all.20.term_ref = f32[8,96,128]{2,1,0:T(8,128)S(1)} all-to-all(f32[8,96,128]{2,1,0:T(8,128)S(1)} %add.11), channel_id=1, replica_groups=mesh['zl'=6,'core'=2,'zh'=2,'y'=8,'x'=4] {'y'}, dimensions={0} | all-to-all | bytes 786432 | tf_op jit(solution)/shard_map/all_to_all | solution.py:175
  101.0 39.1 %all_to_all.21 = f32[12,48,128]{2,1,0:T(8,128)S(1)} all-to-all(f32[12,48,128]{2,1,0:T(8,128)S(1)} %shard_map.41), channel_id=1, replica_groups=mesh['zl'=6,'core'=2,'zh'=2,'y'=8,'x'=4] {'zh','zl'}, dimensions={0} | all-to-all | bytes 589824 | tf_op jit(solution)/shard_map/all_to_all | solution.py:175
  140.1 7.1 %all_to_all.22.parts_ref = f32[2,48,128]{2,1,0:T(8,128)S(1)} all-to-all(f32[2,48,128]{2,1,0:T(8,128)S(1)} %broadcast_in_dim.3), channel_id=1, replica_groups=mesh['zl'=6,'core'=2,'zh'=2,'y'=8,'x'=4] {'core'}, dimensions={0} | all-to-all | bytes 98304 | tf_op jit(solution)/shard_map/all_to_all | solution.py:175
  147.2 0.7 shard_map.42
  (4 shorter events, 0.1 us)
Async XLA Ops:
  0.1 1.1 copy-start.1
  1.1 0.7 copy-start.2
  1.8 26.3 %copy-start = (bf16[1,384,1728]{1,2,0:T(8,128)(2,1)S(1)}, bf16[1,384,1728]{1,2,0:T(8,128)(2,1)}, u32[]{:S(2)}) copy-start(bf16[1,384,1728]{1,2,0:T(8,128)(2,1)} %param.5) | copy-start | bytes 3981316
  4.2 46.7 %copy-start.3 = (s32[1,64]{1,0:T(1,128)S(1)}, s32[1,64]{1,0:T(1,128)}, u32[]{:S(2)}) copy-start(s32[1,64]{1,0:T(1,128)} %counts_ref.3) | copy-start | bytes 772
  4.2 46.7 %all-to-all-start = ((bf16[64,56,128]{2,1,0:T(8,128)(2,1)}), bf16[64,56,128]{2,1,0:T(8,128)(2,1)S(1)}, u32[]{:S(2)}, u32[]{:S(2)}) async-start(bf16[64,56,128]{2,1,0:T(8,128)(2,1)} %shard_map.38), calls=%async_computation | async-start | bytes 1835008 | tf_op jit(solution)/shard_map/all_to_all | solution.py:175
  30.4 29.2 %collective-permute-start = (bf16[2,256,384]{2,1,0:T(8,128)(2,1)}, bf16[2,256,384]{2,1,0:T(8,128)(2,1)S(1)}, u32[]{:S(2)}, u32[]{:S(2)}) collective-permute-start(bf16[2,256,384]{2,1,0:T(8,128)(2,1)} %get-tuple-element.12), channel_id=1, source_target_pairs={{0,1},{1,2},{2,3},{3,0},{4,5},{5,6},{6,7},{7,4},{8,9},{9,10},{10,1... | collective-permute-start | bytes 1179656 | tf_op jit(solution)/shard_map/ppermute | solution.py:180
  33.3 28.8 %collective-permute-start.1 = (bf16[2,256,384]{2,1,0:T(8,128)(2,1)S(1)}, bf16[2,256,384]{2,1,0:T(8,128)(2,1)S(1)}, u32[]{:S(2)}, u32[]{:S(2)}) collective-permute-start(bf16[2,256,384]{2,1,0:T(8,128)(2,1)S(1)} %get-tuple-element.13), channel_id=1, source_target_pairs={{0,2},{1,3},{2,0},{3,1},{4,6},{5,7},{6,4},{7,5},{8,10},{9,11},{10,... | collective-permute-start | bytes 1179656 | tf_op jit(solution)/shard_map/ppermute | solution.py:180
  37.6 24.5 %collective-permute-start.2 = (bf16[2,256,384]{2,1,0:T(8,128)(2,1)S(1)}, bf16[2,256,384]{2,1,0:T(8,128)(2,1)S(1)}, u32[]{:S(2)}, u32[]{:S(2)}) collective-permute-start(bf16[2,256,384]{2,1,0:T(8,128)(2,1)S(1)} %get-tuple-element.14), channel_id=1, source_target_pairs={{0,3},{1,0},{2,1},{3,2},{4,7},{5,4},{6,5},{7,6},{8,11},{9,8},{10,9... | collective-permute-start | bytes 1179656 | tf_op jit(solution)/shard_map/ppermute | solution.py:180
  53.3 14.3 %collective-permute-start.5 = (bf16[400,384]{1,0:T(8,128)(2,1)S(1)}, bf16[400,384]{1,0:T(8,128)(2,1)S(1)}, u32[]{:S(2)}, u32[]{:S(2)}) collective-permute-start(bf16[400,384]{1,0:T(8,128)(2,1)S(1)} %shard_map.39.refs_4_), channel_id=1, source_target_pairs={{0,3},{1,0},{2,1},{3,2},{4,7},{5,4},{6,5},{7,6},{8,11},{9,8},{10,9... | collective-permute-start | bytes 921608 | tf_op jit(solution)/shard_map/ppermute | solution.py:180
  57.7 9.9 %collective-permute-start.4 = (bf16[400,384]{1,0:T(8,128)(2,1)S(1)}, bf16[400,384]{1,0:T(8,128)(2,1)S(1)}, u32[]{:S(2)}, u32[]{:S(2)}) collective-permute-start(bf16[400,384]{1,0:T(8,128)(2,1)S(1)} %shard_map.39.refs_4_), channel_id=1, source_target_pairs={{0,2},{1,3},{2,0},{3,1},{4,6},{5,7},{6,4},{7,5},{8,10},{9,11},{10,... | collective-permute-start | bytes 921608 | tf_op jit(solution)/shard_map/ppermute | solution.py:180
  59.6 16.6 %collective-permute-start.3 = (bf16[400,384]{1,0:T(8,128)(2,1)S(1)}, bf16[400,384]{1,0:T(8,128)(2,1)S(1)}, u32[]{:S(2)}, u32[]{:S(2)}) collective-permute-start(bf16[400,384]{1,0:T(8,128)(2,1)S(1)} %shard_map.39.refs_4_), channel_id=1, source_target_pairs={{0,1},{1,2},{2,3},{3,0},{4,5},{5,6},{6,7},{7,4},{8,9},{9,10},{10,1... | collective-permute-start | bytes 921608 | tf_op jit(solution)/shard_map/ppermute | solution.py:180
  78.4 4.3 %collective-permute-start.6 = (f32[8,96,128]{2,1,0:T(8,128)S(1)}, f32[8,96,128]{2,1,0:T(8,128)S(1)}, u32[]{:S(2)}, u32[]{:S(2)}) collective-permute-start(f32[8,96,128]{2,1,0:T(8,128)S(1)} %get-tuple-element.16), channel_id=1, source_target_pairs={{0,64},{64,0},{1,65},{65,1},{2,66},{66,2},{3,67},{67,3},{4,68},{68... | collective-permute-start | bytes 1179656 | tf_op jit(solution)/shard_map/ppermute | solution.py:180

commit v3 on v2

v3 whole, which is shorter than its diff:
```python
import jax
import jax.numpy as jnp
from jax import lax
from jax.experimental import pallas as pl
from jax.experimental.pallas import tpu as pltpu
from jax.sharding import Mesh
from jax.sharding import PartitionSpec as P


BLK = 16
LANES = 128
TILES = 3
REST = 8
PAIRS = TILES * BLK // 2 + 1
PART = 16
HALF = TILES * PART
ENC = ("zh", "y", "x")
Z = ("zh", "zl")
DP = ("zl", "core")
FIRST = 3
MIB = 1024 * 1024


def pack_kernel(at_ref, pix_ref, out_ref, rows_ref):
    n_enc = out_ref.shape[0]
    whole, patches = rows_ref.shape[1], pix_ref.shape[1]
    me = at_ref[0]
    start = lax.fori_loop(
        0,
        n_enc,
        lambda e, total: total + jnp.where(e < me, at_ref[FIRST + e], 0),
        0,
        unroll=8,
    )
    side = 256
    eye = (
        lax.broadcasted_iota(jnp.int32, (side, side), 0)
        == lax.broadcasted_iota(jnp.int32, (side, side), 1)
    ).astype(jnp.bfloat16)
    for b in range(patches // side):
        turned = lax.dot_general(
            eye,
            pix_ref[:whole, b * side : (b + 1) * side],
            (((1,), (1,)), ((), ())),
            preferred_element_type=jnp.float32,
        )
        rows_ref[b * side : (b + 1) * side, :] = turned.astype(jnp.bfloat16)
    column = lax.broadcasted_iota(jnp.int32, (REST, LANES), 0)
    mine = lax.broadcasted_iota(jnp.int32, (REST, LANES), 1) // BLK == column
    per_tile = LANES // BLK
    rests = []
    for tile in range(patches // LANES):
        rest = pix_ref[whole:, tile * LANES : (tile + 1) * LANES].astype(jnp.float32)
        rests.append(pltpu.roll(rest, 0, 1, stride=BLK, stride_axis=0))
    for s in range(patches // BLK):
        t = lax.rem(start + s, n_enc)
        for j in range(TILES):
            block = rows_ref[s * BLK : (s + 1) * BLK, j * LANES : (j + 1) * LANES]
            out_ref[t, j * BLK // 2 : (j + 1) * BLK // 2] = block.reshape(BLK // 2, 2, LANES)
        rest = pltpu.roll(rests[s // per_tile], -s % per_tile * BLK, 1)
        row = jnp.sum(jnp.where(mine, rest, 0.0), axis=0, keepdims=True)
        out_ref[t, PAIRS - 1] = jnp.broadcast_to(row, (2, LANES)).astype(jnp.bfloat16)


def cut_kernel(at_ref, cot_ref, *refs):
    *out_refs, from_ref, wide_ref, cut_ref = refs
    nx, _, rows, _ = cut_ref.shape
    shards = rows // PART
    own = cot_ref.shape[0] // (nx * shards)
    step = cot_ref.shape[0] // 4
    for m in range(4):
        at = slice(m * step, (m + 1) * step)
        wide_ref[at, :] = cot_ref[at, :].astype(jnp.float32)

    def cut(pair, _):
        base = pl.multiple_of(pair * (2 * nx * own), 8)
        for zh in range(2):
            for b in range(2 * nx):
                to = pl.multiple_of(pair * (4 * PART), PART) + (b // nx * 2 + zh) * PART
                for c in range(2):
                    first = zh * nx * (shards // 2) * own + b * own + c * (own - PART)
                    low = first // 8 * 8
                    span = pl.cdiv(first - low + PART, 8) * 8
                    part = wide_ref[pl.ds(pl.multiple_of(base + low, 8), span), :][
                        first - low : first - low + PART
                    ]
                    cut_ref[b % nx, c, pl.ds(pl.multiple_of(to, PART), PART), :] = part.astype(
                        jnp.bfloat16
                    )
        return 0

    lax.fori_loop(0, shards // 4, cut, 0)
    for d, out_ref in enumerate(out_refs):
        out_ref[...] = cut_ref[lax.rem(at_ref[2] + d, nx)]
    n_enc = nx * shards

    def trace(e, start):
        count = at_ref[FIRST + e]
        slot = lax.rem(at_ref[0] - lax.rem(start, n_enc) + n_enc, n_enc)

        @pl.when(slot < count)
        def _():
            from_ref[(start + slot) // n_enc] = e

        return start + count

    lax.fori_loop(0, n_enc, trace, 0)


def place_kernel(from_ref, arrived_ref, out_ref):
    depth = out_ref.shape[1]
    column = lax.broadcasted_iota(jnp.int32, (REST, LANES), 0)
    lane = lax.broadcasted_iota(jnp.int32, (REST, LANES), 1)
    per_tile = LANES // BLK
    rests = []
    for k in range(depth // BLK):
        e = from_ref[k]
        for j in range(TILES):
            block = arrived_ref[e, j * BLK // 2 : (j + 1) * BLK // 2]
            out_ref[k * BLK : (k + 1) * BLK, j * LANES : (j + 1) * LANES] = block.reshape(
                BLK, LANES
            )
        row = arrived_ref[e, PAIRS - 1].astype(jnp.float32)[:1]
        here = k % per_tile
        moved = pltpu.roll(jnp.broadcast_to(row, (REST, LANES)), here * BLK, 1)
        for by in (1, 2, 4):
            back = pltpu.roll(moved, LANES - by * BLK, 1)
            moved = jnp.where(column // by % 2 == 1, back, moved)
        if here == 0:
            rests.append(moved)
        else:
            rests[-1] = jnp.where(lane // BLK == here, moved, rests[-1])
    rest = jnp.concatenate(rests, axis=1)
    out_ref[depth:, :] = jnp.concatenate([rest, rest], axis=0).astype(jnp.bfloat16)


def grad_kernel(at_ref, *refs):
    keep_ref, send_ref, sums_ref = refs[-3:]
    nx = (len(refs) - 3) // 2
    cut_refs, pix_refs = refs[:nx], refs[nx : 2 * nx]
    rows, depth = cut_refs[0].shape[1:]
    for c in range(2):
        whole = rest = 0.0
        for cut_ref, pix_ref in zip(cut_refs, pix_refs):
            cut = cut_ref[c]
            whole += jnp.dot(cut, pix_ref[:depth, :], preferred_element_type=jnp.float32)
            spread = jnp.concatenate([pix_ref[depth:, :]] * (LANES // (2 * REST)), axis=0)
            rest += lax.dot_general(
                cut, spread, (((1,), (1,)), ((), ())), preferred_element_type=jnp.float32
            )
        sums_ref[c, :, : TILES * LANES] = whole
        sums_ref[c, :, TILES * LANES :] = rest
    place = lax.broadcasted_iota(jnp.int32, (PART, LANES), 0)
    mine = lax.broadcasted_iota(jnp.int32, (PART, LANES), 1) // REST == place
    for out_ref, c in ((keep_ref, at_ref[1]), (send_ref, 1 - at_ref[1])):
        spare = jnp.where(c == 0, PART - 1, 0)
        for q in range(rows // PART):
            y, zh = q // 2, q % 2
            at = slice(q * PART, (q + 1) * PART)
            row = jnp.sum(
                jnp.where(mine, sums_ref[c, at, TILES * LANES :], 0.0), axis=0, keepdims=True
            )
            for j in range(TILES):
                tile = sums_ref[c, at, j * LANES : (j + 1) * LANES]
                if j == 0:
                    tile = jnp.where(place == spare, row, tile)
                out_ref[y, zh * HALF + j * PART : zh * HALF + (j + 1) * PART, :] = tile


def unpack_kernel(parts_ref, out_ref):
    own = out_ref.shape[0]
    cut = own // 2 + 1
    for c, low, high, first in ((0, 0, cut, 0), (1, cut, own, own - PART)):
        for j in range(TILES):
            tile = jnp.concatenate([parts_ref[4 * j + c], parts_ref[4 * j + 2 + c]], axis=0)
            out_ref[low:high, j * LANES : (j + 1) * LANES] = tile[low - first : high - first]
            if j == 0:
                spare = PART - 1 if c == 0 else 0
                row = tile[spare : spare + 1]
        for r in range(low, high):
            out_ref[r : r + 1, TILES * LANES :] = row[:, (r - first) * REST : (r - first + 1) * REST]


def exchange(value, axes):
    return lax.all_to_all(value, axes, split_axis=0, concat_axis=0, tiled=True)


def shift(value, axis, by):
    size = lax.axis_size(axis)
    return lax.ppermute(value, axis, [(i, (i + by) % size) for i in range(size)])


def call(kernel, out_shape, scratch, args, mib):
    spaces = [pltpu.SMEM if a.dtype == jnp.int32 else pltpu.VMEM for a in args]
    outs = jax.tree.map(
        lambda o: pl.BlockSpec(memory_space=pltpu.SMEM if o.dtype == jnp.int32 else pltpu.VMEM),
        out_shape,
    )
    return pl.pallas_call(
        kernel,
        out_shape=out_shape,
        in_specs=[pl.BlockSpec(memory_space=space) for space in spaces],
        out_specs=outs,
        scratch_shapes=scratch,
        compiler_params=pltpu.CompilerParams(vmem_limit_bytes=mib * MIB),
        cost_estimate=pl.CostEstimate(flops=0, bytes_accessed=6 * MIB, transcendentals=0),
    )(*args)


def gradient(counts, pixels, cotangent):
    n_enc, n_dp, nz = lax.axis_size(ENC), lax.axis_size(DP), lax.axis_size(Z)
    nx, ny = lax.axis_size("x"), lax.axis_size("y")
    at = [lax.axis_index(ENC), lax.axis_index("core"), lax.axis_index("x")]
    at = jnp.concatenate([jnp.stack(at).astype(jnp.int32), counts[0]])
    pix, cot = pixels[0].T, cotangent[0].T
    width, depth = cot.shape
    bf16 = lambda *shape: jax.ShapeDtypeStruct(shape, jnp.bfloat16)
    f32 = lambda *shape: jax.ShapeDtypeStruct(shape, jnp.float32)
    rows = 2 * ny * PART

    messages = call(
        pack_kernel,
        bf16(n_enc, PAIRS, 2, LANES),
        [pltpu.VMEM((pix.shape[1], TILES * LANES), jnp.bfloat16)],
        (at, pix),
        8,
    )
    arrived = exchange(messages, ENC)
    *cuts, source = call(
        cut_kernel,
        [bf16(2, rows, depth)] * nx + [jax.ShapeDtypeStruct((depth // BLK,), jnp.int32)],
        [pltpu.VMEM((width, depth), jnp.float32), pltpu.VMEM((nx, 2, rows, depth), jnp.bfloat16)],
        (at, cot),
        12,
    )
    cuts = [cuts[0]] + [shift(cuts[d], "x", d) for d in range(1, nx)]
    placed = call(
        place_kernel, bf16(depth + 2 * REST, TILES * LANES), [], (source, arrived), 8
    )
    row = [placed] + [shift(placed, "x", d) for d in range(1, nx)]
    keep, send = call(
        grad_kernel,
        [f32(ny, 2 * HALF, LANES)] * 2,
        [pltpu.VMEM((2, rows, (TILES + 1) * LANES), jnp.float32)],
        (at, *cuts, *row),
        16,
    )
    terms = keep + shift(send, "core", 1)
    terms = jnp.sum(exchange(terms, "y"), axis=0)
    terms = jnp.sum(exchange(terms.reshape(nz, -1, LANES), Z), axis=0)
    parts = exchange(jnp.broadcast_to(terms, (n_dp, *terms.shape)), DP)
    return call(unpack_kernel, f32(width // n_enc, pix.shape[0]), [], (parts,), 8)


def solution(mesh):
    torus = Mesh(mesh.devices.reshape(6, 2, 2, 8, 4), ("zl", "core", "zh", "y", "x"))
    return jax.shard_map(
        gradient,
        mesh=torus,
        in_specs=(P(DP, None), P(DP, ENC, None), P(DP, ENC, None)),
        out_specs=P(ENC, None),
        check_vma=False,
    )
```

time: 148 us -> 146 us (0.986)
  waiting for transfers between devices: 25.6 us -> 22.8 us
    all_to_all x1, waiting for transfers between devices: 10.2 us -> 7.35 us  [exchange(): return lax.all_to_all(value, axes, split_axis=0, concat_axis=0, tiled=True)]
    pallas_call x6 -> x5, Pallas kernels: 9.95 us -> 9.8 us  [call(): pl.pallas_call(kernel, out_shape=out_shape, in_specs=[pl.BlockSpec(memory...]
  transfers between devices with their start and end apart: 8 -> 8, of which waited for: 4 -> 6; matrix products, arithmetic and copies ran while one was open for 0% -> 0% of each run, Pallas kernels for 3% -> 3%
where the time goes in v3:
time: 146 us; the launch traced here: 145 us
  blocking collectives  64.4 us (44%)
  starting transfers between devices  46.1 us (32%)
  waiting for transfers between devices  22.8 us (16%)
  Pallas kernels  9.8 us (7%)
    all_to_all x3, blocking collectives, exchange(): return lax.all_to_all(value, axes, split_axis=0, concat_axis=0, tiled=True)  64.4 us
    all_to_all x1, starting transfers between devices, exchange(): return lax.all_to_all(value, axes, split_axis=0, concat_axis=0, tiled=True)  23.8 us
    ppermute x7, starting transfers between devices, shift(): lax.ppermute(value, axis, [(i, (i + by) % size) for i in range(size)])  22.3 us
    ppermute x7, waiting for transfers between devices, shift(): lax.ppermute(value, axis, [(i, (i + by) % size) for i in range(size)])  15.4 us
    pallas_call x5, Pallas kernels, call(): pl.pallas_call(kernel, out_shape=out_shape, in_specs=[pl.BlockSpec(memory...  9.8 us
    all_to_all x1, waiting for transfers between devices, exchange(): return lax.all_to_all(value, axes, split_axis=0, concat_axis=0, tiled=True)  7.35 us
  transfers between devices with their start and end apart: 8, of which 6 were waited for; matrix products, arithmetic and copies ran while one was open for 0% of the time, Pallas kernels for 3%

profile of v3, /device:TPU:1, one launch (start us, length us, event | category | flops | bytes accessed | tf_op | source)
XLA Modules:
  0.0 145.0 jit_solution(14613297409032485027)
XLA Ops:
  0.0 0.7 pad_add_fusion.at_ref
  0.7 0.0 copy-start.1
  0.7 1.1 copy-done.1
  1.8 0.0 copy-start
  1.8 2.3 %shard_map.38 = bf16[64,25,2,128]{3,2,1,0:T(2,128)(2,1)} custom-call(s32[67]{0:T(128)S(1)} %pad_add_fusion.at_ref, bf16[392,768]{1,0:T(8,128)(2,1)S(1)} %bitcast.12), custom_call_target="tpu_custom_call" | custom-call | bytes 6291456 | tf_op jit(solution)/shard_map/pallas_call | solution.py:199
  4.2 23.8 %all-to-all-start = ((bf16[64,25,2,128]{3,2,1,0:T(2,128)(2,1)}), bf16[64,25,2,128]{3,2,1,0:T(2,128)(2,1)S(1)}, u32[]{:S(2)}, u32[]{:S(2)}) async-start(bf16[64,25,2,128]{3,2,1,0:T(2,128)(2,1)} %shard_map.38), calls=%async_computation | async-start | bytes 1638400 | tf_op jit(solution)/shard_map/all_to_all | solution.py:185
  27.9 0.0 copy-done
  27.9 3.6 %shard_map.37 = (bf16[2,256,384]{2,1,0:T(8,128)(2,1)S(1)}, bf16[2,256,384]{2,1,0:T(8,128)(2,1)}, bf16[2,256,384]{2,1,0:T(8,128)(2,1)S(1)}, bf16[2,256,384]{2,1,0:T(8,128)(2,1)S(1)}, s32[24]{0:T(128)S(1)}) custom-call(s32[67]{0:T(128)S(1)} %pad_add_fusion.at_ref, bf16[1728,384]{1,0:T(8,128)(2,1)S(1)} %bitcast.11), custom_call_target="tpu_custom_call" | custom-call | bytes 6291456 | tf_op jit(solution)/shard_map/pallas_call | solution.py:199
  31.5 2.9 %collective-permute-start = (bf16[2,256,384]{2,1,0:T(8,128)(2,1)}, bf16[2,256,384]{2,1,0:T(8,128)(2,1)S(1)}, u32[]{:S(2)}, u32[]{:S(2)}) collective-permute-start(bf16[2,256,384]{2,1,0:T(8,128)(2,1)} %get-tuple-element.13), channel_id=1, source_target_pairs={{0,1},{1,2},{2,3},{3,0},{4,5},{5,6},{6,7},{7,4},{8,9},{9,10},{10,1... | collective-permute-start | bytes 1179656 | tf_op jit(solution)/shard_map/ppermute | solution.py:190
  34.4 4.3 %collective-permute-start.1 = (bf16[2,256,384]{2,1,0:T(8,128)(2,1)S(1)}, bf16[2,256,384]{2,1,0:T(8,128)(2,1)S(1)}, u32[]{:S(2)}, u32[]{:S(2)}) collective-permute-start(bf16[2,256,384]{2,1,0:T(8,128)(2,1)S(1)} %get-tuple-element.14), channel_id=1, source_target_pairs={{0,2},{1,3},{2,0},{3,1},{4,6},{5,7},{6,4},{7,5},{8,10},{9,11},{10,... | collective-permute-start | bytes 1179656 | tf_op jit(solution)/shard_map/ppermute | solution.py:190
  38.8 3.1 %collective-permute-start.2 = (bf16[2,256,384]{2,1,0:T(8,128)(2,1)S(1)}, bf16[2,256,384]{2,1,0:T(8,128)(2,1)S(1)}, u32[]{:S(2)}, u32[]{:S(2)}) collective-permute-start(bf16[2,256,384]{2,1,0:T(8,128)(2,1)S(1)} %get-tuple-element.15), channel_id=1, source_target_pairs={{0,3},{1,0},{2,1},{3,2},{4,7},{5,4},{6,5},{7,6},{8,11},{9,8},{10,9... | collective-permute-start | bytes 1179656 | tf_op jit(solution)/shard_map/ppermute | solution.py:190
  41.9 7.4 %all-to-all-done.arrived_ref = bf16[64,25,2,128]{3,2,1,0:T(2,128)(2,1)S(1)} async-done(((bf16[64,25,2,128]{3,2,1,0:T(2,128)(2,1)}), bf16[64,25,2,128]{3,2,1,0:T(2,128)(2,1)S(1)}, u32[]{:S(2)}, u32[]{:S(2)}) %all-to-all-start) | async-done | bytes 819232 | tf_op jit(solution)/shard_map/all_to_all | solution.py:185
  49.2 1.0 shard_map.39.refs_4_
  50.2 4.3 %collective-permute-start.5 = (bf16[400,384]{1,0:T(8,128)(2,1)S(1)}, bf16[400,384]{1,0:T(8,128)(2,1)S(1)}, u32[]{:S(2)}, u32[]{:S(2)}) collective-permute-start(bf16[400,384]{1,0:T(8,128)(2,1)S(1)} %shard_map.39.refs_4_), channel_id=1, source_target_pairs={{0,3},{1,0},{2,1},{3,2},{4,7},{5,4},{6,5},{7,6},{8,11},{9,8},{10,9... | collective-permute-start | bytes 921608 | tf_op jit(solution)/shard_map/ppermute | solution.py:190
  54.6 1.9 %collective-permute-start.4 = (bf16[400,384]{1,0:T(8,128)(2,1)S(1)}, bf16[400,384]{1,0:T(8,128)(2,1)S(1)}, u32[]{:S(2)}, u32[]{:S(2)}) collective-permute-start(bf16[400,384]{1,0:T(8,128)(2,1)S(1)} %shard_map.39.refs_4_), channel_id=1, source_target_pairs={{0,2},{1,3},{2,0},{3,1},{4,6},{5,7},{6,4},{7,5},{8,10},{9,11},{10,... | collective-permute-start | bytes 921608 | tf_op jit(solution)/shard_map/ppermute | solution.py:190
  56.5 0.0 collective-permute-done.refs_1_
  56.5 2.5 %collective-permute-start.3 = (bf16[400,384]{1,0:T(8,128)(2,1)S(1)}, bf16[400,384]{1,0:T(8,128)(2,1)S(1)}, u32[]{:S(2)}, u32[]{:S(2)}) collective-permute-start(bf16[400,384]{1,0:T(8,128)(2,1)S(1)} %shard_map.39.refs_4_), channel_id=1, source_target_pairs={{0,1},{1,2},{2,3},{3,0},{4,5},{5,6},{6,7},{7,4},{8,9},{9,10},{10,1... | collective-permute-start | bytes 921608 | tf_op jit(solution)/shard_map/ppermute | solution.py:190
  59.0 0.9 collective-permute-done.1.refs_2_
  59.9 0.7 collective-permute-done.2.refs_3_
  60.6 6.6 %collective-permute-done.5.refs_7_ = bf16[400,384]{1,0:T(8,128)(2,1)S(1)} collective-permute-done((bf16[400,384]{1,0:T(8,128)(2,1)S(1)}, bf16[400,384]{1,0:T(8,128)(2,1)S(1)}, u32[]{:S(2)}, u32[]{:S(2)}) %collective-permute-start.5) | collective-permute-done | bytes 307232 | tf_op jit(solution)/shard_map/ppermute | solution.py:190
  67.2 0.0 collective-permute-done.4.refs_6_
  67.2 5.9 %collective-permute-done.3.refs_5_ = bf16[400,384]{1,0:T(8,128)(2,1)S(1)} collective-permute-done((bf16[400,384]{1,0:T(8,128)(2,1)S(1)}, bf16[400,384]{1,0:T(8,128)(2,1)S(1)}, u32[]{:S(2)}, u32[]{:S(2)}) %collective-permute-start.3) | collective-permute-done | bytes 307232 | tf_op jit(solution)/shard_map/ppermute | solution.py:190
  73.1 2.2 %shard_map.40 = (f32[8,96,128]{2,1,0:T(8,128)S(1)}, f32[8,96,128]{2,1,0:T(8,128)S(1)}) custom-call(s32[67]{0:T(128)S(1)} %pad_add_fusion.at_ref, bf16[2,256,384]{2,1,0:T(8,128)(2,1)S(1)} %get-tuple-element.12.refs_0_, bf16[2,256,384]{2,1,0:T(8,128)(2,1)S(1)} %collective-permute-done.refs_1_, bf16[2,256,384]{2,1,0:T(8,128)(2,1)S(1)} %collective-permute-done.1.refs_2_, ...), custom_call_target="tpu_custom_call" | custom-call | bytes 6291456 | tf_op jit(solution)/shard_map/pallas_call | solution.py:199
  75.3 3.3 %collective-permute-start.6 = (f32[8,96,128]{2,1,0:T(8,128)S(1)}, f32[8,96,128]{2,1,0:T(8,128)S(1)}, u32[]{:S(2)}, u32[]{:S(2)}) collective-permute-start(f32[8,96,128]{2,1,0:T(8,128)S(1)} %get-tuple-element.18), channel_id=1, source_target_pairs={{0,64},{64,0},{1,65},{65,1},{2,66},{66,2},{3,67},{67,3},{4,68},{68... | collective-permute-start | bytes 1179656 | tf_op jit(solution)/shard_map/ppermute | solution.py:190
  78.5 1.3 collective-permute-done.6
  79.9 19.8 %all_to_all.20 = f32[8,96,128]{2,1,0:T(8,128)S(1)} all-to-all(f32[8,96,128]{2,1,0:T(8,128)S(1)} %add.11), channel_id=1, replica_groups=mesh['zl'=6,'core'=2,'zh'=2,'y'=8,'x'=4] {'y'}, dimensions={0} | all-to-all | bytes 786432 | tf_op jit(solution)/shard_map/all_to_all | solution.py:185
  99.7 30.5 %all_to_all.21 = f32[12,8,128]{2,1,0:T(8,128)S(1)} all-to-all(f32[12,8,128]{2,1,0:T(8,128)S(1)} %bitcast.13), channel_id=1, replica_groups=mesh['zl'=6,'core'=2,'zh'=2,'y'=8,'x'=4] {'zh','zl'}, dimensions={0} | all-to-all | bytes 98304 | tf_op jit(solution)/shard_map/all_to_all | solution.py:185
  130.2 14.1 %all_to_all.22.parts_ref = f32[12,8,128]{2,1,0:T(8,128)S(1)} all-to-all(f32[12,8,128]{2,1,0:T(8,128)S(1)} %broadcast_in_dim.3), channel_id=1, replica_groups=mesh['zl'=6,'core'=2,'zh'=2,'y'=8,'x'=4] {'zl','core'}, dimensions={0} | all-to-all | bytes 98304 | tf_op jit(solution)/shard_map/all_to_all | solution.py:185
  144.3 0.7 shard_map.41
  (4 shorter events, 0.1 us)
Async XLA Ops:
  0.7 1.1 copy-start.1
  1.8 26.1 %copy-start = (bf16[1,384,1728]{1,2,0:T(8,128)(2,1)S(1)}, bf16[1,384,1728]{1,2,0:T(8,128)(2,1)}, u32[]{:S(2)}) copy-start(bf16[1,384,1728]{1,2,0:T(8,128)(2,1)} %param.5) | copy-start | bytes 3981316
  4.2 45.1 %all-to-all-start = ((bf16[64,25,2,128]{3,2,1,0:T(2,128)(2,1)}), bf16[64,25,2,128]{3,2,1,0:T(2,128)(2,1)S(1)}, u32[]{:S(2)}, u32[]{:S(2)}) async-start(bf16[64,25,2,128]{3,2,1,0:T(2,128)(2,1)} %shard_map.38), calls=%async_computation | async-start | bytes 1638400 | tf_op jit(solution)/shard_map/all_to_all | solution.py:185
  31.5 25.0 %collective-permute-start = (bf16[2,256,384]{2,1,0:T(8,128)(2,1)}, bf16[2,256,384]{2,1,0:T(8,128)(2,1)S(1)}, u32[]{:S(2)}, u32[]{:S(2)}) collective-permute-start(bf16[2,256,384]{2,1,0:T(8,128)(2,1)} %get-tuple-element.13), channel_id=1, source_target_pairs={{0,1},{1,2},{2,3},{3,0},{4,5},{5,6},{6,7},{7,4},{8,9},{9,10},{10,1... | collective-permute-start | bytes 1179656 | tf_op jit(solution)/shard_map/ppermute | solution.py:190
  34.4 25.5 %collective-permute-start.1 = (bf16[2,256,384]{2,1,0:T(8,128)(2,1)S(1)}, bf16[2,256,384]{2,1,0:T(8,128)(2,1)S(1)}, u32[]{:S(2)}, u32[]{:S(2)}) collective-permute-start(bf16[2,256,384]{2,1,0:T(8,128)(2,1)S(1)} %get-tuple-element.14), channel_id=1, source_target_pairs={{0,2},{1,3},{2,0},{3,1},{4,6},{5,7},{6,4},{7,5},{8,10},{9,11},{10,... | collective-permute-start | bytes 1179656 | tf_op jit(solution)/shard_map/ppermute | solution.py:190
  38.8 21.9 %collective-permute-start.2 = (bf16[2,256,384]{2,1,0:T(8,128)(2,1)S(1)}, bf16[2,256,384]{2,1,0:T(8,128)(2,1)S(1)}, u32[]{:S(2)}, u32[]{:S(2)}) collective-permute-start(bf16[2,256,384]{2,1,0:T(8,128)(2,1)S(1)} %get-tuple-element.15), channel_id=1, source_target_pairs={{0,3},{1,0},{2,1},{3,2},{4,7},{5,4},{6,5},{7,6},{8,11},{9,8},{10,9... | collective-permute-start | bytes 1179656 | tf_op jit(solution)/shard_map/ppermute | solution.py:190
  50.2 17.0 %collective-permute-start.5 = (bf16[400,384]{1,0:T(8,128)(2,1)S(1)}, bf16[400,384]{1,0:T(8,128)(2,1)S(1)}, u32[]{:S(2)}, u32[]{:S(2)}) collective-permute-start(bf16[400,384]{1,0:T(8,128)(2,1)S(1)} %shard_map.39.refs_4_), channel_id=1, source_target_pairs={{0,3},{1,0},{2,1},{3,2},{4,7},{5,4},{6,5},{7,6},{8,11},{9,8},{10,9... | collective-permute-start | bytes 921608 | tf_op jit(solution)/shard_map/ppermute | solution.py:190
  54.6 12.7 %collective-permute-start.4 = (bf16[400,384]{1,0:T(8,128)(2,1)S(1)}, bf16[400,384]{1,0:T(8,128)(2,1)S(1)}, u32[]{:S(2)}, u32[]{:S(2)}) collective-permute-start(bf16[400,384]{1,0:T(8,128)(2,1)S(1)} %shard_map.39.refs_4_), channel_id=1, source_target_pairs={{0,2},{1,3},{2,0},{3,1},{4,6},{5,7},{6,4},{7,5},{8,10},{9,11},{10,... | collective-permute-start | bytes 921608 | tf_op jit(solution)/shard_map/ppermute | solution.py:190
  56.5 16.6 %collective-permute-start.3 = (bf16[400,384]{1,0:T(8,128)(2,1)S(1)}, bf16[400,384]{1,0:T(8,128)(2,1)S(1)}, u32[]{:S(2)}, u32[]{:S(2)}) collective-permute-start(bf16[400,384]{1,0:T(8,128)(2,1)S(1)} %shard_map.39.refs_4_), channel_id=1, source_target_pairs={{0,1},{1,2},{2,3},{3,0},{4,5},{5,6},{6,7},{7,4},{8,9},{9,10},{10,1... | collective-permute-start | bytes 921608 | tf_op jit(solution)/shard_map/ppermute | solution.py:190
  75.3 4.6 %collective-permute-start.6 = (f32[8,96,128]{2,1,0:T(8,128)S(1)}, f32[8,96,128]{2,1,0:T(8,128)S(1)}, u32[]{:S(2)}, u32[]{:S(2)}) collective-permute-start(f32[8,96,128]{2,1,0:T(8,128)S(1)} %get-tuple-element.18), channel_id=1, source_target_pairs={{0,64},{64,0},{1,65},{65,1},{2,66},{66,2},{3,67},{67,3},{4,68},{68... | collective-permute-start | bytes 1179656 | tf_op jit(solution)/shard_map/ppermute | solution.py:190

commit v4 on v3

--- a/solution.py
+++ b/solution.py
@@ -63,7 +63,7 @@
 
 
 def cut_kernel(at_ref, cot_ref, *refs):
-    *out_refs, from_ref, wide_ref, cut_ref = refs
+    *out_refs, wide_ref, cut_ref = refs
     nx, _, rows, _ = cut_ref.shape
     shards = rows // PART
     own = cot_ref.shape[0] // (nx * shards)
@@ -92,7 +92,10 @@
     lax.fori_loop(0, shards // 4, cut, 0)
     for d, out_ref in enumerate(out_refs):
         out_ref[...] = cut_ref[lax.rem(at_ref[2] + d, nx)]
-    n_enc = nx * shards
+
+
+def trace_kernel(at_ref, from_ref):
+    n_enc = at_ref.shape[0] - FIRST
 
     def trace(e, start):
         count = at_ref[FIRST + e]
@@ -108,7 +111,7 @@
 
 
 def place_kernel(from_ref, arrived_ref, out_ref):
-    depth = out_ref.shape[1]
+    depth = out_ref.shape[2]
     column = lax.broadcasted_iota(jnp.int32, (REST, LANES), 0)
     lane = lax.broadcasted_iota(jnp.int32, (REST, LANES), 1)
     per_tile = LANES // BLK
@@ -117,7 +120,7 @@
         e = from_ref[k]
         for j in range(TILES):
             block = arrived_ref[e, j * BLK // 2 : (j + 1) * BLK // 2]
-            out_ref[k * BLK : (k + 1) * BLK, j * LANES : (j + 1) * LANES] = block.reshape(
+            out_ref[0, k * BLK : (k + 1) * BLK, j * LANES : (j + 1) * LANES] = block.reshape(
                 BLK, LANES
             )
         row = arrived_ref[e, PAIRS - 1].astype(jnp.float32)[:1]
@@ -131,20 +134,23 @@
         else:
             rests[-1] = jnp.where(lane // BLK == here, moved, rests[-1])
     rest = jnp.concatenate(rests, axis=1)
-    out_ref[depth:, :] = jnp.concatenate([rest, rest], axis=0).astype(jnp.bfloat16)
+    out_ref[0, depth:, :] = jnp.concatenate([rest, rest], axis=0).astype(jnp.bfloat16)
+    for i in range(1, out_ref.shape[0]):
+        out_ref[i] = out_ref[0]
 
 
 def grad_kernel(at_ref, *refs):
     keep_ref, send_ref, sums_ref = refs[-3:]
-    nx = (len(refs) - 3) // 2
-    cut_refs, pix_refs = refs[:nx], refs[nx : 2 * nx]
+    *cut_refs, pix_ref = refs[:-3]
+    nx = len(cut_refs)
     rows, depth = cut_refs[0].shape[1:]
     for c in range(2):
         whole = rest = 0.0
-        for cut_ref, pix_ref in zip(cut_refs, pix_refs):
+        for d, cut_ref in enumerate(cut_refs):
+            came = lax.rem(at_ref[2] + nx - d, nx)
             cut = cut_ref[c]
-            whole += jnp.dot(cut, pix_ref[:depth, :], preferred_element_type=jnp.float32)
-            spread = jnp.concatenate([pix_ref[depth:, :]] * (LANES // (2 * REST)), axis=0)
+            whole += jnp.dot(cut, pix_ref[came, :depth, :], preferred_element_type=jnp.float32)
+            spread = jnp.concatenate([pix_ref[came, depth:, :]] * (LANES // (2 * REST)), axis=0)
             rest += lax.dot_general(
                 cut, spread, (((1,), (1,)), ((), ())), preferred_element_type=jnp.float32
             )
@@ -226,28 +232,27 @@
         8,
     )
     arrived = exchange(messages, ENC)
-    *cuts, source = call(
+    cuts = call(
         cut_kernel,
-        [bf16(2, rows, depth)] * nx + [jax.ShapeDtypeStruct((depth // BLK,), jnp.int32)],
+        [bf16(2, rows, depth)] * nx,
         [pltpu.VMEM((width, depth), jnp.float32), pltpu.VMEM((nx, 2, rows, depth), jnp.bfloat16)],
         (at, cot),
         12,
     )
     cuts = [cuts[0]] + [shift(cuts[d], "x", d) for d in range(1, nx)]
-    placed = call(
-        place_kernel, bf16(depth + 2 * REST, TILES * LANES), [], (source, arrived), 8
-    )
-    row = [placed] + [shift(placed, "x", d) for d in range(1, nx)]
+    source = call(trace_kernel, jax.ShapeDtypeStruct((depth // BLK,), jnp.int32), [], (at,), 1)
+    placed = call(place_kernel, bf16(nx, depth + 2 * REST, TILES * LANES), [], (source, arrived), 8)
+    placed, cuts = lax.optimization_barrier((placed, cuts))
+    row = exchange(placed, "x")
     keep, send = call(
         grad_kernel,
         [f32(ny, 2 * HALF, LANES)] * 2,
         [pltpu.VMEM((2, rows, (TILES + 1) * LANES), jnp.float32)],
-        (at, *cuts, *row),
+        (at, *cuts, row),
         16,
     )
     terms = keep + shift(send, "core", 1)
-    terms = jnp.sum(exchange(terms, "y"), axis=0)
-    terms = jnp.sum(exchange(terms.reshape(nz, -1, LANES), Z), axis=0)
+    terms = jnp.sum(exchange(terms.reshape(ny * nz, -1, LANES), ("y", *Z)), axis=0)
     parts = exchange(jnp.broadcast_to(terms, (n_dp, *terms.shape)), DP)
     return call(unpack_kernel, f32(width // n_enc, pix.shape[0]), [], (parts,), 8)
 

time: 146 us -> 141 us (0.966)
  starting transfers between devices: 46.1 us -> 38.3 us
  blocking collectives: 64.4 us -> 72.2 us
  waiting for transfers between devices: 22.8 us -> 16.8 us
    all_to_all x3, blocking collectives: 64.4 us -> 72.2 us  [exchange(): return lax.all_to_all(value, axes, split_axis=0, concat_axis=0, tiled=True)]
    ppermute x7 -> x4, starting transfers between devices: 22.3 us -> 14.6 us  [shift(): lax.ppermute(value, axis, [(i, (i + by) % size) for i in range(size)])]
    ppermute x7 -> x4, waiting for transfers between devices: 15.4 us -> 10.6 us  [shift(): lax.ppermute(value, axis, [(i, (i + by) % size) for i in range(size)])]
    pallas_call x5 -> x6, Pallas kernels: 9.8 us -> 11 us  [call(): pl.pallas_call(kernel, out_shape=out_shape, in_specs=[pl.BlockSpec(memory...]
  transfers between devices with their start and end apart: 8 -> 5, of which waited for: 6 -> 4; matrix products, arithmetic and copies ran while one was open for 0% -> 0% of each run, Pallas kernels for 3% -> 4%
where the time goes in v4:
time: 141 us; the launch traced here: 140 us
  blocking collectives  72.2 us (51%)
  starting transfers between devices  38.3 us (27%)
  waiting for transfers between devices  16.8 us (12%)
  Pallas kernels  11 us (8%)
    all_to_all x3, blocking collectives, exchange(): return lax.all_to_all(value, axes, split_axis=0, concat_axis=0, tiled=True)  72.2 us
    all_to_all x1, starting transfers between devices, exchange(): return lax.all_to_all(value, axes, split_axis=0, concat_axis=0, tiled=True)  23.8 us
    ppermute x4, starting transfers between devices, shift(): lax.ppermute(value, axis, [(i, (i + by) % size) for i in range(size)])  14.6 us
    pallas_call x6, Pallas kernels, call(): pl.pallas_call(kernel, out_shape=out_shape, in_specs=[pl.BlockSpec(memory...  11 us
    ppermute x4, waiting for transfers between devices, shift(): lax.ppermute(value, axis, [(i, (i + by) % size) for i in range(size)])  10.6 us
    all_to_all x1, waiting for transfers between devices, exchange(): return lax.all_to_all(value, axes, split_axis=0, concat_axis=0, tiled=True)  6.24 us
  transfers between devices with their start and end apart: 5, of which 4 were waited for; matrix products, arithmetic and copies ran while one was open for 0% of the time, Pallas kernels for 4%

profile of v4, /device:TPU:1, one launch (start us, length us, event | category | flops | bytes accessed | tf_op | source)
XLA Modules:
  0.0 140.4 jit_solution(14231916709684541423)
XLA Ops:
  0.0 0.7 pad_add_fusion.at_ref
  0.7 0.0 copy-start.1
  0.7 1.1 copy-done.1
  1.8 0.0 copy-start
  1.8 2.3 %shard_map.38 = bf16[64,25,2,128]{3,2,1,0:T(2,128)(2,1)} custom-call(s32[67]{0:T(128)S(1)} %pad_add_fusion.at_ref, bf16[392,768]{1,0:T(8,128)(2,1)S(1)} %bitcast.12), custom_call_target="tpu_custom_call" | custom-call | bytes 6291456 | tf_op jit(solution)/shard_map/pallas_call | solution.py:205
  4.2 23.8 %all-to-all-start = ((bf16[64,25,2,128]{3,2,1,0:T(2,128)(2,1)}), bf16[64,25,2,128]{3,2,1,0:T(2,128)(2,1)S(1)}, u32[]{:S(2)}, u32[]{:S(2)}) async-start(bf16[64,25,2,128]{3,2,1,0:T(2,128)(2,1)} %shard_map.38), calls=%async_computation | async-start | bytes 1638400 | tf_op jit(solution)/shard_map/all_to_all | solution.py:191
  27.9 0.0 copy-done
  27.9 2.3 %shard_map.40 = (bf16[2,256,384]{2,1,0:T(8,128)(2,1)S(1)}, bf16[2,256,384]{2,1,0:T(8,128)(2,1)}, bf16[2,256,384]{2,1,0:T(8,128)(2,1)S(1)}, bf16[2,256,384]{2,1,0:T(8,128)(2,1)S(1)}) custom-call(s32[67]{0:T(128)S(1)} %pad_add_fusion.at_ref, bf16[1728,384]{1,0:T(8,128)(2,1)S(1)} %bitcast.11), custom_call_target="tpu_custom_call" | custom-call | bytes 6291456 | tf_op jit(solution)/shard_map/pallas_call | solution.py:205
  30.2 2.9 %collective-permute-start = (bf16[2,256,384]{2,1,0:T(8,128)(2,1)}, bf16[2,256,384]{2,1,0:T(8,128)(2,1)S(1)}, u32[]{:S(2)}, u32[]{:S(2)}) collective-permute-start(bf16[2,256,384]{2,1,0:T(8,128)(2,1)} %get-tuple-element.17), channel_id=1, source_target_pairs={{0,1},{1,2},{2,3},{3,0},{4,5},{5,6},{6,7},{7,4},{8,9},{9,10},{10,1... | collective-permute-start | bytes 1179656 | tf_op jit(solution)/shard_map/ppermute | solution.py:196
  33.1 4.3 %collective-permute-start.1 = (bf16[2,256,384]{2,1,0:T(8,128)(2,1)S(1)}, bf16[2,256,384]{2,1,0:T(8,128)(2,1)S(1)}, u32[]{:S(2)}, u32[]{:S(2)}) collective-permute-start(bf16[2,256,384]{2,1,0:T(8,128)(2,1)S(1)} %get-tuple-element.18), channel_id=1, source_target_pairs={{0,2},{1,3},{2,0},{3,1},{4,6},{5,7},{6,4},{7,5},{8,10},{9,11},{10,... | collective-permute-start | bytes 1179656 | tf_op jit(solution)/shard_map/ppermute | solution.py:196
  37.5 3.1 %collective-permute-start.2 = (bf16[2,256,384]{2,1,0:T(8,128)(2,1)S(1)}, bf16[2,256,384]{2,1,0:T(8,128)(2,1)S(1)}, u32[]{:S(2)}, u32[]{:S(2)}) collective-permute-start(bf16[2,256,384]{2,1,0:T(8,128)(2,1)S(1)} %get-tuple-element.19), channel_id=1, source_target_pairs={{0,3},{1,0},{2,1},{3,2},{4,7},{5,4},{6,5},{7,6},{8,11},{9,8},{10,9... | collective-permute-start | bytes 1179656 | tf_op jit(solution)/shard_map/ppermute | solution.py:196
  40.5 2.4 %shard_map.37.from_ref = s32[24]{0:T(128)S(1)} custom-call(s32[67]{0:T(128)S(1)} %pad_add_fusion.at_ref), custom_call_target="tpu_custom_call" | custom-call | bytes 6291456 | tf_op jit(solution)/shard_map/pallas_call | solution.py:205
  43.0 6.2 %all-to-all-done.arrived_ref = bf16[64,25,2,128]{3,2,1,0:T(2,128)(2,1)S(1)} async-done(((bf16[64,25,2,128]{3,2,1,0:T(2,128)(2,1)}), bf16[64,25,2,128]{3,2,1,0:T(2,128)(2,1)S(1)}, u32[]{:S(2)}, u32[]{:S(2)}) %all-to-all-start) | async-done | bytes 819232 | tf_op jit(solution)/shard_map/all_to_all | solution.py:191
  49.2 1.1 shard_map.39
  50.3 0.0 collective-permute-done.refs_1_
  50.3 9.0 %collective-permute-done.1.refs_2_ = bf16[2,256,384]{2,1,0:T(8,128)(2,1)S(1)} collective-permute-done((bf16[2,256,384]{2,1,0:T(8,128)(2,1)S(1)}, bf16[2,256,384]{2,1,0:T(8,128)(2,1)S(1)}, u32[]{:S(2)}, u32[]{:S(2)}) %collective-permute-start.1) | collective-permute-done | bytes 393248 | tf_op jit(solution)/shard_map/ppermute | solution.py:196
  59.3 0.2 collective-permute-done.2.refs_3_
  59.5 19.5 %all_to_all.20.refs_4_ = bf16[4,400,384]{2,1,0:T(8,128)(2,1)S(1)} all-to-all(bf16[4,400,384]{2,1,0:T(8,128)(2,1)S(1)} %shard_map.39), channel_id=1, replica_groups=mesh['zl'=6,'core'=2,'zh'=2,'y'=8,'x'=4] {'x'}, dimensions={0} | all-to-all | bytes 2457600 | tf_op jit(solution)/shard_map/all_to_all | solution.py:191
  79.1 2.1 %shard_map.41 = (f32[8,96,128]{2,1,0:T(8,128)S(1)}, f32[8,96,128]{2,1,0:T(8,128)S(1)}) custom-call(s32[67]{0:T(128)S(1)} %pad_add_fusion.at_ref, bf16[2,256,384]{2,1,0:T(8,128)(2,1)S(1)} %get-tuple-element.20.refs_0_, bf16[2,256,384]{2,1,0:T(8,128)(2,1)S(1)} %collective-permute-done.refs_1_, bf16[2,256,384]{2,1,0:T(8,128)(2,1)S(1)} %collective-permute-done.1.refs_2_, ...), custom_call_target="tpu_custom_call" | custom-call | bytes 6291456 | tf_op jit(solution)/shard_map/pallas_call | solution.py:205
  81.2 4.3 %collective-permute-start.3 = (f32[8,96,128]{2,1,0:T(8,128)S(1)}, f32[8,96,128]{2,1,0:T(8,128)S(1)}, u32[]{:S(2)}, u32[]{:S(2)}) collective-permute-start(f32[8,96,128]{2,1,0:T(8,128)S(1)} %get-tuple-element.26), channel_id=1, source_target_pairs={{0,64},{64,0},{1,65},{65,1},{2,66},{66,2},{3,67},{67,3},{4,68},{68... | collective-permute-start | bytes 1179656 | tf_op jit(solution)/shard_map/ppermute | solution.py:196
  85.5 1.3 collective-permute-done.3
  86.8 0.1 add.11
  86.9 37.7 %all_to_all.21 = f32[96,8,128]{2,1,0:T(8,128)S(1)} all-to-all(f32[96,8,128]{2,1,0:T(8,128)S(1)} %bitcast.13), channel_id=1, replica_groups=mesh['zl'=6,'core'=2,'zh'=2,'y'=8,'x'=4] {'y','zh','zl'}, dimensions={0} | all-to-all | bytes 786432 | tf_op jit(solution)/shard_map/all_to_all | solution.py:191
  124.6 0.1 reduce_sum.9
  124.7 15.0 %all_to_all.22.parts_ref = f32[12,8,128]{2,1,0:T(8,128)S(1)} all-to-all(f32[12,8,128]{2,1,0:T(8,128)S(1)} %broadcast_in_dim.3), channel_id=1, replica_groups=mesh['zl'=6,'core'=2,'zh'=2,'y'=8,'x'=4] {'zl','core'}, dimensions={0} | all-to-all | bytes 98304 | tf_op jit(solution)/shard_map/all_to_all | solution.py:191
  139.7 0.7 shard_map.42
  (1 shorter events, 0.0 us)
Async XLA Ops:
  0.7 1.1 copy-start.1
  1.8 26.1 %copy-start = (bf16[1,384,1728]{1,2,0:T(8,128)(2,1)S(1)}, bf16[1,384,1728]{1,2,0:T(8,128)(2,1)}, u32[]{:S(2)}) copy-start(bf16[1,384,1728]{1,2,0:T(8,128)(2,1)} %param.5) | copy-start | bytes 3981316
  4.2 45.1 %all-to-all-start = ((bf16[64,25,2,128]{3,2,1,0:T(2,128)(2,1)}), bf16[64,25,2,128]{3,2,1,0:T(2,128)(2,1)S(1)}, u32[]{:S(2)}, u32[]{:S(2)}) async-start(bf16[64,25,2,128]{3,2,1,0:T(2,128)(2,1)} %shard_map.38), calls=%async_computation | async-start | bytes 1638400 | tf_op jit(solution)/shard_map/all_to_all | solution.py:191
  30.2 20.0 %collective-permute-start = (bf16[2,256,384]{2,1,0:T(8,128)(2,1)}, bf16[2,256,384]{2,1,0:T(8,128)(2,1)S(1)}, u32[]{:S(2)}, u32[]{:S(2)}) collective-permute-start(bf16[2,256,384]{2,1,0:T(8,128)(2,1)} %get-tuple-element.17), channel_id=1, source_target_pairs={{0,1},{1,2},{2,3},{3,0},{4,5},{5,6},{6,7},{7,4},{8,9},{9,10},{10,1... | collective-permute-start | bytes 1179656 | tf_op jit(solution)/shard_map/ppermute | solution.py:196
  33.1 26.1 %collective-permute-start.1 = (bf16[2,256,384]{2,1,0:T(8,128)(2,1)S(1)}, bf16[2,256,384]{2,1,0:T(8,128)(2,1)S(1)}, u32[]{:S(2)}, u32[]{:S(2)}) collective-permute-start(bf16[2,256,384]{2,1,0:T(8,128)(2,1)S(1)} %get-tuple-element.18), channel_id=1, source_target_pairs={{0,2},{1,3},{2,0},{3,1},{4,6},{5,7},{6,4},{7,5},{8,10},{9,11},{10,... | collective-permute-start | bytes 1179656 | tf_op jit(solution)/shard_map/ppermute | solution.py:196
  37.5 22.1 %collective-permute-start.2 = (bf16[2,256,384]{2,1,0:T(8,128)(2,1)S(1)}, bf16[2,256,384]{2,1,0:T(8,128)(2,1)S(1)}, u32[]{:S(2)}, u32[]{:S(2)}) collective-permute-start(bf16[2,256,384]{2,1,0:T(8,128)(2,1)S(1)} %get-tuple-element.19), channel_id=1, source_target_pairs={{0,3},{1,0},{2,1},{3,2},{4,7},{5,4},{6,5},{7,6},{8,11},{9,8},{10,9... | collective-permute-start | bytes 1179656 | tf_op jit(solution)/shard_map/ppermute | solution.py:196
  81.2 5.6 %collective-permute-start.3 = (f32[8,96,128]{2,1,0:T(8,128)S(1)}, f32[8,96,128]{2,1,0:T(8,128)S(1)}, u32[]{:S(2)}, u32[]{:S(2)}) collective-permute-start(f32[8,96,128]{2,1,0:T(8,128)S(1)} %get-tuple-element.26), channel_id=1, source_target_pairs={{0,64},{64,0},{1,65},{65,1},{2,66},{66,2},{3,67},{67,3},{4,68},{68... | collective-permute-start | bytes 1179656 | tf_op jit(solution)/shard_map/ppermute | solution.py:196

commit v5 on v4

--- a/solution.py
+++ b/solution.py
@@ -21,23 +21,34 @@
 MIB = 1024 * 1024
 
 
-def pack_kernel(at_ref, pix_ref, out_ref, rows_ref):
+def pack_kernel(me_ref, counts_ref, far_ref, out_ref, rows_ref, pix_ref, sems):
     n_enc = out_ref.shape[0]
     whole, patches = rows_ref.shape[1], pix_ref.shape[1]
-    me = at_ref[0]
+    side = 256
+    copies = [
+        pltpu.make_async_copy(
+            far_ref.at[:, b * side : (b + 1) * side],
+            pix_ref.at[:, b * side : (b + 1) * side],
+            sems.at[b],
+        )
+        for b in range(patches // side)
+    ]
+    for copy in copies:
+        copy.start()
+    me = me_ref[0]
     start = lax.fori_loop(
         0,
         n_enc,
-        lambda e, total: total + jnp.where(e < me, at_ref[FIRST + e], 0),
+        lambda e, total: total + jnp.where(e < me, counts_ref[0, e], 0),
         0,
         unroll=8,
     )
-    side = 256
     eye = (
         lax.broadcasted_iota(jnp.int32, (side, side), 0)
         == lax.broadcasted_iota(jnp.int32, (side, side), 1)
     ).astype(jnp.bfloat16)
     for b in range(patches // side):
+        copies[b].wait()
         turned = lax.dot_general(
             eye,
             pix_ref[:whole, b * side : (b + 1) * side],
@@ -196,8 +207,8 @@
     return lax.ppermute(value, axis, [(i, (i + by) % size) for i in range(size)])
 
 
-def call(kernel, out_shape, scratch, args, mib):
-    spaces = [pltpu.SMEM if a.dtype == jnp.int32 else pltpu.VMEM for a in args]
+def call(kernel, out_shape, scratch, args, mib, space=pltpu.VMEM):
+    spaces = [pltpu.SMEM if a.dtype == jnp.int32 else space for a in args]
     outs = jax.tree.map(
         lambda o: pl.BlockSpec(memory_space=pltpu.SMEM if o.dtype == jnp.int32 else pltpu.VMEM),
         out_shape,
@@ -208,7 +219,7 @@
         in_specs=[pl.BlockSpec(memory_space=space) for space in spaces],
         out_specs=outs,
         scratch_shapes=scratch,
-        compiler_params=pltpu.CompilerParams(vmem_limit_bytes=mib * MIB),
+        compiler_params=pltpu.CompilerParams(vmem_limit_bytes=mib and mib * MIB),
         cost_estimate=pl.CostEstimate(flops=0, bytes_accessed=6 * MIB, transcendentals=0),
     )(*args)
 
@@ -216,6 +227,7 @@
 def gradient(counts, pixels, cotangent):
     n_enc, n_dp, nz = lax.axis_size(ENC), lax.axis_size(DP), lax.axis_size(Z)
     nx, ny = lax.axis_size("x"), lax.axis_size("y")
+    me = lax.axis_index(ENC).astype(jnp.int32)[None]
     at = [lax.axis_index(ENC), lax.axis_index("core"), lax.axis_index("x")]
     at = jnp.concatenate([jnp.stack(at).astype(jnp.int32), counts[0]])
     pix, cot = pixels[0].T, cotangent[0].T
@@ -227,9 +239,14 @@
     messages = call(
         pack_kernel,
         bf16(n_enc, PAIRS, 2, LANES),
-        [pltpu.VMEM((pix.shape[1], TILES * LANES), jnp.bfloat16)],
-        (at, pix),
-        8,
+        [
+            pltpu.VMEM((pix.shape[1], TILES * LANES), jnp.bfloat16),
+            pltpu.VMEM(pix.shape, jnp.bfloat16),
+            pltpu.SemaphoreType.DMA((pix.shape[1] // 256,)),
+        ],
+        (me, counts, pix),
+        None,
+        pltpu.HBM,
     )
     arrived = exchange(messages, ENC)
     cuts = call(

time: 141 us -> 141 us (level)
  Pallas kernels: 11 us -> 12.5 us
    pallas_call x6, Pallas kernels: 11 us -> 12.5 us  [call(): pl.pallas_call(kernel, out_shape=out_shape, in_specs=[pl.BlockSpec(memory...]
where the time goes in v5:
time: 141 us; the launch traced here: 140 us
  blocking collectives  72.2 us (51%)
  starting transfers between devices  38.3 us (27%)
  waiting for transfers between devices  16.8 us (12%)
  Pallas kernels  12.5 us (9%)
    all_to_all x3, blocking collectives, exchange(): return lax.all_to_all(value, axes, split_axis=0, concat_axis=0, tiled=True)  72.2 us
    all_to_all x1, starting transfers between devices, exchange(): return lax.all_to_all(value, axes, split_axis=0, concat_axis=0, tiled=True)  23.8 us
    ppermute x4, starting transfers between devices, shift(): lax.ppermute(value, axis, [(i, (i + by) % size) for i in range(size)])  14.6 us
    pallas_call x6, Pallas kernels, call(): pl.pallas_call(kernel, out_shape=out_shape, in_specs=[pl.BlockSpec(memory...  12.5 us
    ppermute x4, waiting for transfers between devices, shift(): lax.ppermute(value, axis, [(i, (i + by) % size) for i in range(size)])  10.6 us
    all_to_all x1, waiting for transfers between devices, exchange(): return lax.all_to_all(value, axes, split_axis=0, concat_axis=0, tiled=True)  6.18 us
  transfers between devices with their start and end apart: 5, of which 4 were waited for; matrix products, arithmetic and copies ran while one was open for 0% of the time, Pallas kernels for 4%

profile of v5, /device:TPU:1, one launch (start us, length us, event | category | flops | bytes accessed | tf_op | source)
XLA Modules:
  0.0 140.1 jit_solution(2036021569564683048)
XLA Ops:
  0.0 0.0 copy-start.1
  0.0 0.0 copy-start
  0.0 3.8 %shard_map.38 = bf16[64,25,2,128]{3,2,1,0:T(2,128)(2,1)} custom-call(s32[1]{0:T(128)} %bitcast.me_ref, s32[1,64]{1,0:T(1,128)} %counts_ref.1, bf16[392,768]{1,0:T(8,128)(2,1)} %bitcast.13), custom_call_target="tpu_custom_call" | custom-call | bytes 6291456 | tf_op jit(solution)/shard_map/pallas_call | solution.py:216
  3.9 23.8 %all-to-all-start = ((bf16[64,25,2,128]{3,2,1,0:T(2,128)(2,1)}), bf16[64,25,2,128]{3,2,1,0:T(2,128)(2,1)S(1)}, u32[]{:S(2)}, u32[]{:S(2)}) async-start(bf16[64,25,2,128]{3,2,1,0:T(2,128)(2,1)} %shard_map.38), calls=%async_computation | async-start | bytes 1638400 | tf_op jit(solution)/shard_map/all_to_all | solution.py:202
  27.6 0.0 copy-done.1
  27.7 0.1 pad_add_fusion.at_ref
  27.7 0.0 copy-done
  27.7 2.3 %shard_map.40 = (bf16[2,256,384]{2,1,0:T(8,128)(2,1)S(1)}, bf16[2,256,384]{2,1,0:T(8,128)(2,1)}, bf16[2,256,384]{2,1,0:T(8,128)(2,1)S(1)}, bf16[2,256,384]{2,1,0:T(8,128)(2,1)S(1)}) custom-call(s32[67]{0:T(128)S(1)} %pad_add_fusion.at_ref, bf16[1728,384]{1,0:T(8,128)(2,1)S(1)} %bitcast.11), custom_call_target="tpu_custom_call" | custom-call | bytes 6291456 | tf_op jit(solution)/shard_map/pallas_call | solution.py:216
  30.0 2.9 %collective-permute-start = (bf16[2,256,384]{2,1,0:T(8,128)(2,1)}, bf16[2,256,384]{2,1,0:T(8,128)(2,1)S(1)}, u32[]{:S(2)}, u32[]{:S(2)}) collective-permute-start(bf16[2,256,384]{2,1,0:T(8,128)(2,1)} %get-tuple-element.17), channel_id=1, source_target_pairs={{0,1},{1,2},{2,3},{3,0},{4,5},{5,6},{6,7},{7,4},{8,9},{9,10},{10,1... | collective-permute-start | bytes 1179656 | tf_op jit(solution)/shard_map/ppermute | solution.py:207
  32.9 4.3 %collective-permute-start.1 = (bf16[2,256,384]{2,1,0:T(8,128)(2,1)S(1)}, bf16[2,256,384]{2,1,0:T(8,128)(2,1)S(1)}, u32[]{:S(2)}, u32[]{:S(2)}) collective-permute-start(bf16[2,256,384]{2,1,0:T(8,128)(2,1)S(1)} %get-tuple-element.18), channel_id=1, source_target_pairs={{0,2},{1,3},{2,0},{3,1},{4,6},{5,7},{6,4},{7,5},{8,10},{9,11},{10,... | collective-permute-start | bytes 1179656 | tf_op jit(solution)/shard_map/ppermute | solution.py:207
  37.2 3.1 %collective-permute-start.2 = (bf16[2,256,384]{2,1,0:T(8,128)(2,1)S(1)}, bf16[2,256,384]{2,1,0:T(8,128)(2,1)S(1)}, u32[]{:S(2)}, u32[]{:S(2)}) collective-permute-start(bf16[2,256,384]{2,1,0:T(8,128)(2,1)S(1)} %get-tuple-element.19), channel_id=1, source_target_pairs={{0,3},{1,0},{2,1},{3,2},{4,7},{5,4},{6,5},{7,6},{8,11},{9,8},{10,9... | collective-permute-start | bytes 1179656 | tf_op jit(solution)/shard_map/ppermute | solution.py:207
  40.3 2.4 %shard_map.37.from_ref = s32[24]{0:T(128)S(1)} custom-call(s32[67]{0:T(128)S(1)} %pad_add_fusion.at_ref), custom_call_target="tpu_custom_call" | custom-call | bytes 6291456 | tf_op jit(solution)/shard_map/pallas_call | solution.py:216
  42.8 6.2 %all-to-all-done.arrived_ref = bf16[64,25,2,128]{3,2,1,0:T(2,128)(2,1)S(1)} async-done(((bf16[64,25,2,128]{3,2,1,0:T(2,128)(2,1)}), bf16[64,25,2,128]{3,2,1,0:T(2,128)(2,1)S(1)}, u32[]{:S(2)}, u32[]{:S(2)}) %all-to-all-start) | async-done | bytes 819232 | tf_op jit(solution)/shard_map/all_to_all | solution.py:202
  48.9 1.0 shard_map.39
  50.0 0.0 collective-permute-done.refs_1_
  50.0 9.0 %collective-permute-done.1.refs_2_ = bf16[2,256,384]{2,1,0:T(8,128)(2,1)S(1)} collective-permute-done((bf16[2,256,384]{2,1,0:T(8,128)(2,1)S(1)}, bf16[2,256,384]{2,1,0:T(8,128)(2,1)S(1)}, u32[]{:S(2)}, u32[]{:S(2)}) %collective-permute-start.1) | collective-permute-done | bytes 393248 | tf_op jit(solution)/shard_map/ppermute | solution.py:207
  59.0 0.3 collective-permute-done.2.refs_3_
  59.3 19.6 %all_to_all.20.refs_4_ = bf16[4,400,384]{2,1,0:T(8,128)(2,1)S(1)} all-to-all(bf16[4,400,384]{2,1,0:T(8,128)(2,1)S(1)} %shard_map.39), channel_id=1, replica_groups=mesh['zl'=6,'core'=2,'zh'=2,'y'=8,'x'=4] {'x'}, dimensions={0} | all-to-all | bytes 2457600 | tf_op jit(solution)/shard_map/all_to_all | solution.py:202
  78.9 2.2 %shard_map.41 = (f32[8,96,128]{2,1,0:T(8,128)S(1)}, f32[8,96,128]{2,1,0:T(8,128)S(1)}) custom-call(s32[67]{0:T(128)S(1)} %pad_add_fusion.at_ref, bf16[2,256,384]{2,1,0:T(8,128)(2,1)S(1)} %get-tuple-element.20.refs_0_, bf16[2,256,384]{2,1,0:T(8,128)(2,1)S(1)} %collective-permute-done.refs_1_, bf16[2,256,384]{2,1,0:T(8,128)(2,1)S(1)} %collective-permute-done.1.refs_2_, ...), custom_call_target="tpu_custom_call" | custom-call | bytes 6291456 | tf_op jit(solution)/shard_map/pallas_call | solution.py:216
  81.0 4.3 %collective-permute-start.3 = (f32[8,96,128]{2,1,0:T(8,128)S(1)}, f32[8,96,128]{2,1,0:T(8,128)S(1)}, u32[]{:S(2)}, u32[]{:S(2)}) collective-permute-start(f32[8,96,128]{2,1,0:T(8,128)S(1)} %get-tuple-element.26), channel_id=1, source_target_pairs={{0,64},{64,0},{1,65},{65,1},{2,66},{66,2},{3,67},{67,3},{4,68},{68... | collective-permute-start | bytes 1179656 | tf_op jit(solution)/shard_map/ppermute | solution.py:207
  85.3 1.3 collective-permute-done.3
  86.6 0.1 add.13
  86.7 37.6 %all_to_all.21 = f32[96,8,128]{2,1,0:T(8,128)S(1)} all-to-all(f32[96,8,128]{2,1,0:T(8,128)S(1)} %bitcast.12), channel_id=1, replica_groups=mesh['zl'=6,'core'=2,'zh'=2,'y'=8,'x'=4] {'y','zh','zl'}, dimensions={0} | all-to-all | bytes 786432 | tf_op jit(solution)/shard_map/all_to_all | solution.py:202
  124.3 0.1 reduce_sum.9
  124.4 15.0 %all_to_all.22.parts_ref = f32[12,8,128]{2,1,0:T(8,128)S(1)} all-to-all(f32[12,8,128]{2,1,0:T(8,128)S(1)} %broadcast_in_dim.4), channel_id=1, replica_groups=mesh['zl'=6,'core'=2,'zh'=2,'y'=8,'x'=4] {'zl','core'}, dimensions={0} | all-to-all | bytes 98304 | tf_op jit(solution)/shard_map/all_to_all | solution.py:202
  139.4 0.7 shard_map.42
  (1 shorter events, 0.0 us)
Async XLA Ops:
  0.0 27.6 %copy-start.1 = (s32[1,64]{1,0:T(1,128)S(1)}, s32[1,64]{1,0:T(1,128)}, u32[]{:S(2)}) copy-start(s32[1,64]{1,0:T(1,128)} %counts_ref.1) | copy-start | bytes 772
  0.0 27.7 %copy-start = (bf16[1,384,1728]{1,2,0:T(8,128)(2,1)S(1)}, bf16[1,384,1728]{1,2,0:T(8,128)(2,1)}, u32[]{:S(2)}) copy-start(bf16[1,384,1728]{1,2,0:T(8,128)(2,1)} %param.5) | copy-start | bytes 3981316
  3.9 45.1 %all-to-all-start = ((bf16[64,25,2,128]{3,2,1,0:T(2,128)(2,1)}), bf16[64,25,2,128]{3,2,1,0:T(2,128)(2,1)S(1)}, u32[]{:S(2)}, u32[]{:S(2)}) async-start(bf16[64,25,2,128]{3,2,1,0:T(2,128)(2,1)} %shard_map.38), calls=%async_computation | async-start | bytes 1638400 | tf_op jit(solution)/shard_map/all_to_all | solution.py:202
  30.0 20.0 %collective-permute-start = (bf16[2,256,384]{2,1,0:T(8,128)(2,1)}, bf16[2,256,384]{2,1,0:T(8,128)(2,1)S(1)}, u32[]{:S(2)}, u32[]{:S(2)}) collective-permute-start(bf16[2,256,384]{2,1,0:T(8,128)(2,1)} %get-tuple-element.17), channel_id=1, source_target_pairs={{0,1},{1,2},{2,3},{3,0},{4,5},{5,6},{6,7},{7,4},{8,9},{9,10},{10,1... | collective-permute-start | bytes 1179656 | tf_op jit(solution)/shard_map/ppermute | solution.py:207
  32.9 26.1 %collective-permute-start.1 = (bf16[2,256,384]{2,1,0:T(8,128)(2,1)S(1)}, bf16[2,256,384]{2,1,0:T(8,128)(2,1)S(1)}, u32[]{:S(2)}, u32[]{:S(2)}) collective-permute-start(bf16[2,256,384]{2,1,0:T(8,128)(2,1)S(1)} %get-tuple-element.18), channel_id=1, source_target_pairs={{0,2},{1,3},{2,0},{3,1},{4,6},{5,7},{6,4},{7,5},{8,10},{9,11},{10,... | collective-permute-start | bytes 1179656 | tf_op jit(solution)/shard_map/ppermute | solution.py:207
  37.2 22.1 %collective-permute-start.2 = (bf16[2,256,384]{2,1,0:T(8,128)(2,1)S(1)}, bf16[2,256,384]{2,1,0:T(8,128)(2,1)S(1)}, u32[]{:S(2)}, u32[]{:S(2)}) collective-permute-start(bf16[2,256,384]{2,1,0:T(8,128)(2,1)S(1)} %get-tuple-element.19), channel_id=1, source_target_pairs={{0,3},{1,0},{2,1},{3,2},{4,7},{5,4},{6,5},{7,6},{8,11},{9,8},{10,9... | collective-permute-start | bytes 1179656 | tf_op jit(solution)/shard_map/ppermute | solution.py:207
  81.0 5.6 %collective-permute-start.3 = (f32[8,96,128]{2,1,0:T(8,128)S(1)}, f32[8,96,128]{2,1,0:T(8,128)S(1)}, u32[]{:S(2)}, u32[]{:S(2)}) collective-permute-start(f32[8,96,128]{2,1,0:T(8,128)S(1)} %get-tuple-element.26), channel_id=1, source_target_pairs={{0,64},{64,0},{1,65},{65,1},{2,66},{66,2},{3,67},{67,3},{4,68},{68... | collective-permute-start | bytes 1179656 | tf_op jit(solution)/shard_map/ppermute | solution.py:207

commit v6 on v4

--- a/solution.py
+++ b/solution.py
@@ -21,22 +21,25 @@
 MIB = 1024 * 1024
 
 
-def pack_kernel(at_ref, pix_ref, out_ref, rows_ref):
+def pack_kernel(me_ref, counts_ref, pix_ref, out_ref, rows_ref):
     n_enc = out_ref.shape[0]
     whole, patches = rows_ref.shape[1], pix_ref.shape[1]
-    me = at_ref[0]
+    side = 256
+    me = me_ref[0]
     start = lax.fori_loop(
         0,
         n_enc,
-        lambda e, total: total + jnp.where(e < me, at_ref[FIRST + e], 0),
+        lambda e, total: total + jnp.where(e < me, counts_ref[0, e], 0),
         0,
         unroll=8,
     )
-    side = 256
     eye = (
         lax.broadcasted_iota(jnp.int32, (side, side), 0)
         == lax.broadcasted_iota(jnp.int32, (side, side), 1)
     ).astype(jnp.bfloat16)
+    column = lax.broadcasted_iota(jnp.int32, (REST, LANES), 0)
+    mine = lax.broadcasted_iota(jnp.int32, (REST, LANES), 1) // BLK == column
+    per_tile = LANES // BLK
     for b in range(patches // side):
         turned = lax.dot_general(
             eye,
@@ -45,21 +48,19 @@
             preferred_element_type=jnp.float32,
         )
         rows_ref[b * side : (b + 1) * side, :] = turned.astype(jnp.bfloat16)
-    column = lax.broadcasted_iota(jnp.int32, (REST, LANES), 0)
-    mine = lax.broadcasted_iota(jnp.int32, (REST, LANES), 1) // BLK == column
-    per_tile = LANES // BLK
-    rests = []
-    for tile in range(patches // LANES):
-        rest = pix_ref[whole:, tile * LANES : (tile + 1) * LANES].astype(jnp.float32)
-        rests.append(pltpu.roll(rest, 0, 1, stride=BLK, stride_axis=0))
-    for s in range(patches // BLK):
-        t = lax.rem(start + s, n_enc)
-        for j in range(TILES):
-            block = rows_ref[s * BLK : (s + 1) * BLK, j * LANES : (j + 1) * LANES]
-            out_ref[t, j * BLK // 2 : (j + 1) * BLK // 2] = block.reshape(BLK // 2, 2, LANES)
-        rest = pltpu.roll(rests[s // per_tile], -s % per_tile * BLK, 1)
-        row = jnp.sum(jnp.where(mine, rest, 0.0), axis=0, keepdims=True)
-        out_ref[t, PAIRS - 1] = jnp.broadcast_to(row, (2, LANES)).astype(jnp.bfloat16)
+        rests = []
+        for tile in range(b * side // LANES, (b + 1) * side // LANES):
+            rest = pix_ref[whole:, tile * LANES : (tile + 1) * LANES].astype(jnp.float32)
+            rests.append(pltpu.roll(rest, 0, 1, stride=BLK, stride_axis=0))
+        for i in range(side // BLK):
+            s = b * (side // BLK) + i
+            t = lax.rem(start + s, n_enc)
+            for j in range(TILES):
+                block = rows_ref[s * BLK : (s + 1) * BLK, j * LANES : (j + 1) * LANES]
+                out_ref[t, j * BLK // 2 : (j + 1) * BLK // 2] = block.reshape(BLK // 2, 2, LANES)
+            rest = pltpu.roll(rests[i // per_tile], -i % per_tile * BLK, 1)
+            row = jnp.sum(jnp.where(mine, rest, 0.0), axis=0, keepdims=True)
+            out_ref[t, PAIRS - 1] = jnp.broadcast_to(row, (2, LANES)).astype(jnp.bfloat16)
 
 
 def cut_kernel(at_ref, cot_ref, *refs):
@@ -208,7 +209,7 @@
         in_specs=[pl.BlockSpec(memory_space=space) for space in spaces],
         out_specs=outs,
         scratch_shapes=scratch,
-        compiler_params=pltpu.CompilerParams(vmem_limit_bytes=mib * MIB),
+        compiler_params=pltpu.CompilerParams(vmem_limit_bytes=mib and mib * MIB),
         cost_estimate=pl.CostEstimate(flops=0, bytes_accessed=6 * MIB, transcendentals=0),
     )(*args)
 
@@ -216,6 +217,7 @@
 def gradient(counts, pixels, cotangent):
     n_enc, n_dp, nz = lax.axis_size(ENC), lax.axis_size(DP), lax.axis_size(Z)
     nx, ny = lax.axis_size("x"), lax.axis_size("y")
+    me = lax.axis_index(ENC).astype(jnp.int32)[None]
     at = [lax.axis_index(ENC), lax.axis_index("core"), lax.axis_index("x")]
     at = jnp.concatenate([jnp.stack(at).astype(jnp.int32), counts[0]])
     pix, cot = pixels[0].T, cotangent[0].T
@@ -228,8 +230,8 @@
         pack_kernel,
         bf16(n_enc, PAIRS, 2, LANES),
         [pltpu.VMEM((pix.shape[1], TILES * LANES), jnp.bfloat16)],
-        (at, pix),
-        8,
+        (me, counts, pix),
+        None,
     )
     arrived = exchange(messages, ENC)
     cuts = call(

time: 141 us -> 140 us (level)
  no operation moved by 1% of the time
where the time goes in v6:
time: 140 us; the launch traced here: 139 us
  blocking collectives  72.2 us (52%)
  starting transfers between devices  38.3 us (27%)
  waiting for transfers between devices  16.8 us (12%)
  Pallas kernels  11.6 us (8%)
    all_to_all x3, blocking collectives, exchange(): return lax.all_to_all(value, axes, split_axis=0, concat_axis=0, tiled=True)  72.2 us
    all_to_all x1, starting transfers between devices, exchange(): return lax.all_to_all(value, axes, split_axis=0, concat_axis=0, tiled=True)  23.8 us
    ppermute x4, starting transfers between devices, shift(): lax.ppermute(value, axis, [(i, (i + by) % size) for i in range(size)])  14.6 us
    pallas_call x6, Pallas kernels, call(): pl.pallas_call(kernel, out_shape=out_shape, in_specs=[pl.BlockSpec(memory...  11.6 us
    ppermute x4, waiting for transfers between devices, shift(): lax.ppermute(value, axis, [(i, (i + by) % size) for i in range(size)])  10.6 us
    all_to_all x1, waiting for transfers between devices, exchange(): return lax.all_to_all(value, axes, split_axis=0, concat_axis=0, tiled=True)  6.17 us
  transfers between devices with their start and end apart: 5, of which 4 were waited for; matrix products, arithmetic and copies ran while one was open for 0% of the time, Pallas kernels for 4%

profile of v6, /device:TPU:1, one launch (start us, length us, event | category | flops | bytes accessed | tf_op | source)
XLA Modules:
  0.0 139.3 jit_solution(7380107827995998002)
XLA Ops:
  0.0 0.0 copy-start.1
  0.0 0.0 copy-start
  0.0 3.0 %shard_map.38 = bf16[64,25,2,128]{3,2,1,0:T(2,128)(2,1)} custom-call(s32[1]{0:T(128)} %bitcast.me_ref, s32[1,64]{1,0:T(1,128)} %counts_ref.1, bf16[392,768]{1,0:T(8,128)(2,1)} %bitcast.13), custom_call_target="tpu_custom_call" | custom-call | bytes 6291456 | tf_op jit(solution)/shard_map/pallas_call | solution.py:206
  3.0 23.8 %all-to-all-start = ((bf16[64,25,2,128]{3,2,1,0:T(2,128)(2,1)}), bf16[64,25,2,128]{3,2,1,0:T(2,128)(2,1)S(1)}, u32[]{:S(2)}, u32[]{:S(2)}) async-start(bf16[64,25,2,128]{3,2,1,0:T(2,128)(2,1)} %shard_map.38), calls=%async_computation | async-start | bytes 1638400 | tf_op jit(solution)/shard_map/all_to_all | solution.py:192
  26.8 0.0 copy-done.1
  26.8 0.1 pad_add_fusion.at_ref
  26.9 0.0 copy-done
  26.9 2.3 %shard_map.40 = (bf16[2,256,384]{2,1,0:T(8,128)(2,1)S(1)}, bf16[2,256,384]{2,1,0:T(8,128)(2,1)}, bf16[2,256,384]{2,1,0:T(8,128)(2,1)S(1)}, bf16[2,256,384]{2,1,0:T(8,128)(2,1)S(1)}) custom-call(s32[67]{0:T(128)S(1)} %pad_add_fusion.at_ref, bf16[1728,384]{1,0:T(8,128)(2,1)S(1)} %bitcast.11), custom_call_target="tpu_custom_call" | custom-call | bytes 6291456 | tf_op jit(solution)/shard_map/pallas_call | solution.py:206
  29.1 2.9 %collective-permute-start = (bf16[2,256,384]{2,1,0:T(8,128)(2,1)}, bf16[2,256,384]{2,1,0:T(8,128)(2,1)S(1)}, u32[]{:S(2)}, u32[]{:S(2)}) collective-permute-start(bf16[2,256,384]{2,1,0:T(8,128)(2,1)} %get-tuple-element.17), channel_id=1, source_target_pairs={{0,1},{1,2},{2,3},{3,0},{4,5},{5,6},{6,7},{7,4},{8,9},{9,10},{10,1... | collective-permute-start | bytes 1179656 | tf_op jit(solution)/shard_map/ppermute | solution.py:197
  32.1 4.3 %collective-permute-start.1 = (bf16[2,256,384]{2,1,0:T(8,128)(2,1)S(1)}, bf16[2,256,384]{2,1,0:T(8,128)(2,1)S(1)}, u32[]{:S(2)}, u32[]{:S(2)}) collective-permute-start(bf16[2,256,384]{2,1,0:T(8,128)(2,1)S(1)} %get-tuple-element.18), channel_id=1, source_target_pairs={{0,2},{1,3},{2,0},{3,1},{4,6},{5,7},{6,4},{7,5},{8,10},{9,11},{10,... | collective-permute-start | bytes 1179656 | tf_op jit(solution)/shard_map/ppermute | solution.py:197
  36.4 3.1 %collective-permute-start.2 = (bf16[2,256,384]{2,1,0:T(8,128)(2,1)S(1)}, bf16[2,256,384]{2,1,0:T(8,128)(2,1)S(1)}, u32[]{:S(2)}, u32[]{:S(2)}) collective-permute-start(bf16[2,256,384]{2,1,0:T(8,128)(2,1)S(1)} %get-tuple-element.19), channel_id=1, source_target_pairs={{0,3},{1,0},{2,1},{3,2},{4,7},{5,4},{6,5},{7,6},{8,11},{9,8},{10,9... | collective-permute-start | bytes 1179656 | tf_op jit(solution)/shard_map/ppermute | solution.py:197
  39.5 2.4 %shard_map.37.from_ref = s32[24]{0:T(128)S(1)} custom-call(s32[67]{0:T(128)S(1)} %pad_add_fusion.at_ref), custom_call_target="tpu_custom_call" | custom-call | bytes 6291456 | tf_op jit(solution)/shard_map/pallas_call | solution.py:206
  41.9 6.2 %all-to-all-done.arrived_ref = bf16[64,25,2,128]{3,2,1,0:T(2,128)(2,1)S(1)} async-done(((bf16[64,25,2,128]{3,2,1,0:T(2,128)(2,1)}), bf16[64,25,2,128]{3,2,1,0:T(2,128)(2,1)S(1)}, u32[]{:S(2)}, u32[]{:S(2)}) %all-to-all-start) | async-done | bytes 819232 | tf_op jit(solution)/shard_map/all_to_all | solution.py:192
  48.1 1.0 shard_map.39
  49.1 0.0 collective-permute-done.refs_1_
  49.1 9.0 %collective-permute-done.1.refs_2_ = bf16[2,256,384]{2,1,0:T(8,128)(2,1)S(1)} collective-permute-done((bf16[2,256,384]{2,1,0:T(8,128)(2,1)S(1)}, bf16[2,256,384]{2,1,0:T(8,128)(2,1)S(1)}, u32[]{:S(2)}, u32[]{:S(2)}) %collective-permute-start.1) | collective-permute-done | bytes 393248 | tf_op jit(solution)/shard_map/ppermute | solution.py:197
  58.1 0.3 collective-permute-done.2.refs_3_
  58.4 19.6 %all_to_all.20.refs_4_ = bf16[4,400,384]{2,1,0:T(8,128)(2,1)S(1)} all-to-all(bf16[4,400,384]{2,1,0:T(8,128)(2,1)S(1)} %shard_map.39), channel_id=1, replica_groups=mesh['zl'=6,'core'=2,'zh'=2,'y'=8,'x'=4] {'x'}, dimensions={0} | all-to-all | bytes 2457600 | tf_op jit(solution)/shard_map/all_to_all | solution.py:192
  78.0 2.2 %shard_map.41 = (f32[8,96,128]{2,1,0:T(8,128)S(1)}, f32[8,96,128]{2,1,0:T(8,128)S(1)}) custom-call(s32[67]{0:T(128)S(1)} %pad_add_fusion.at_ref, bf16[2,256,384]{2,1,0:T(8,128)(2,1)S(1)} %get-tuple-element.20.refs_0_, bf16[2,256,384]{2,1,0:T(8,128)(2,1)S(1)} %collective-permute-done.refs_1_, bf16[2,256,384]{2,1,0:T(8,128)(2,1)S(1)} %collective-permute-done.1.refs_2_, ...), custom_call_target="tpu_custom_call" | custom-call | bytes 6291456 | tf_op jit(solution)/shard_map/pallas_call | solution.py:206
  80.2 4.3 %collective-permute-start.3 = (f32[8,96,128]{2,1,0:T(8,128)S(1)}, f32[8,96,128]{2,1,0:T(8,128)S(1)}, u32[]{:S(2)}, u32[]{:S(2)}) collective-permute-start(f32[8,96,128]{2,1,0:T(8,128)S(1)} %get-tuple-element.26), channel_id=1, source_target_pairs={{0,64},{64,0},{1,65},{65,1},{2,66},{66,2},{3,67},{67,3},{4,68},{68... | collective-permute-start | bytes 1179656 | tf_op jit(solution)/shard_map/ppermute | solution.py:197
  84.4 1.3 collective-permute-done.3
  85.8 0.1 add.13
  85.8 37.6 %all_to_all.21 = f32[96,8,128]{2,1,0:T(8,128)S(1)} all-to-all(f32[96,8,128]{2,1,0:T(8,128)S(1)} %bitcast.12), channel_id=1, replica_groups=mesh['zl'=6,'core'=2,'zh'=2,'y'=8,'x'=4] {'y','zh','zl'}, dimensions={0} | all-to-all | bytes 786432 | tf_op jit(solution)/shard_map/all_to_all | solution.py:192
  123.4 0.1 reduce_sum.9
  123.5 15.0 %all_to_all.22.parts_ref = f32[12,8,128]{2,1,0:T(8,128)S(1)} all-to-all(f32[12,8,128]{2,1,0:T(8,128)S(1)} %broadcast_in_dim.4), channel_id=1, replica_groups=mesh['zl'=6,'core'=2,'zh'=2,'y'=8,'x'=4] {'zl','core'}, dimensions={0} | all-to-all | bytes 98304 | tf_op jit(solution)/shard_map/all_to_all | solution.py:192
  138.5 0.7 shard_map.42
  (1 shorter events, 0.0 us)
Async XLA Ops:
  0.0 26.8 %copy-start.1 = (s32[1,64]{1,0:T(1,128)S(1)}, s32[1,64]{1,0:T(1,128)}, u32[]{:S(2)}) copy-start(s32[1,64]{1,0:T(1,128)} %counts_ref.1) | copy-start | bytes 772
  0.0 26.9 %copy-start = (bf16[1,384,1728]{1,2,0:T(8,128)(2,1)S(1)}, bf16[1,384,1728]{1,2,0:T(8,128)(2,1)}, u32[]{:S(2)}) copy-start(bf16[1,384,1728]{1,2,0:T(8,128)(2,1)} %param.5) | copy-start | bytes 3981316
  3.0 45.1 %all-to-all-start = ((bf16[64,25,2,128]{3,2,1,0:T(2,128)(2,1)}), bf16[64,25,2,128]{3,2,1,0:T(2,128)(2,1)S(1)}, u32[]{:S(2)}, u32[]{:S(2)}) async-start(bf16[64,25,2,128]{3,2,1,0:T(2,128)(2,1)} %shard_map.38), calls=%async_computation | async-start | bytes 1638400 | tf_op jit(solution)/shard_map/all_to_all | solution.py:192
  29.1 20.0 %collective-permute-start = (bf16[2,256,384]{2,1,0:T(8,128)(2,1)}, bf16[2,256,384]{2,1,0:T(8,128)(2,1)S(1)}, u32[]{:S(2)}, u32[]{:S(2)}) collective-permute-start(bf16[2,256,384]{2,1,0:T(8,128)(2,1)} %get-tuple-element.17), channel_id=1, source_target_pairs={{0,1},{1,2},{2,3},{3,0},{4,5},{5,6},{6,7},{7,4},{8,9},{9,10},{10,1... | collective-permute-start | bytes 1179656 | tf_op jit(solution)/shard_map/ppermute | solution.py:197
  32.1 26.1 %collective-permute-start.1 = (bf16[2,256,384]{2,1,0:T(8,128)(2,1)S(1)}, bf16[2,256,384]{2,1,0:T(8,128)(2,1)S(1)}, u32[]{:S(2)}, u32[]{:S(2)}) collective-permute-start(bf16[2,256,384]{2,1,0:T(8,128)(2,1)S(1)} %get-tuple-element.18), channel_id=1, source_target_pairs={{0,2},{1,3},{2,0},{3,1},{4,6},{5,7},{6,4},{7,5},{8,10},{9,11},{10,... | collective-permute-start | bytes 1179656 | tf_op jit(solution)/shard_map/ppermute | solution.py:197
  36.4 22.0 %collective-permute-start.2 = (bf16[2,256,384]{2,1,0:T(8,128)(2,1)S(1)}, bf16[2,256,384]{2,1,0:T(8,128)(2,1)S(1)}, u32[]{:S(2)}, u32[]{:S(2)}) collective-permute-start(bf16[2,256,384]{2,1,0:T(8,128)(2,1)S(1)} %get-tuple-element.19), channel_id=1, source_target_pairs={{0,3},{1,0},{2,1},{3,2},{4,7},{5,4},{6,5},{7,6},{8,11},{9,8},{10,9... | collective-permute-start | bytes 1179656 | tf_op jit(solution)/shard_map/ppermute | solution.py:197
  80.2 5.6 %collective-permute-start.3 = (f32[8,96,128]{2,1,0:T(8,128)S(1)}, f32[8,96,128]{2,1,0:T(8,128)S(1)}, u32[]{:S(2)}, u32[]{:S(2)}) collective-permute-start(f32[8,96,128]{2,1,0:T(8,128)S(1)} %get-tuple-element.26), channel_id=1, source_target_pairs={{0,64},{64,0},{1,65},{65,1},{2,66},{66,2},{3,67},{67,3},{4,68},{68... | collective-permute-start | bytes 1179656 | tf_op jit(solution)/shard_map/ppermute | solution.py:197

commit v7 on v6

--- a/solution.py
+++ b/solution.py
@@ -21,9 +21,9 @@
 MIB = 1024 * 1024
 
 
-def pack_kernel(me_ref, counts_ref, pix_ref, out_ref, rows_ref):
+def pack_kernel(me_ref, counts_ref, pix_ref, out_ref):
     n_enc = out_ref.shape[0]
-    whole, patches = rows_ref.shape[1], pix_ref.shape[1]
+    whole, patches = TILES * LANES, pix_ref.shape[1]
     side = 256
     me = me_ref[0]
     start = lax.fori_loop(
@@ -47,7 +47,7 @@
             (((1,), (1,)), ((), ())),
             preferred_element_type=jnp.float32,
         )
-        rows_ref[b * side : (b + 1) * side, :] = turned.astype(jnp.bfloat16)
+        turned = turned.astype(jnp.bfloat16)
         rests = []
         for tile in range(b * side // LANES, (b + 1) * side // LANES):
             rest = pix_ref[whole:, tile * LANES : (tile + 1) * LANES].astype(jnp.float32)
@@ -56,7 +56,7 @@
             s = b * (side // BLK) + i
             t = lax.rem(start + s, n_enc)
             for j in range(TILES):
-                block = rows_ref[s * BLK : (s + 1) * BLK, j * LANES : (j + 1) * LANES]
+                block = turned[i * BLK : (i + 1) * BLK, j * LANES : (j + 1) * LANES]
                 out_ref[t, j * BLK // 2 : (j + 1) * BLK // 2] = block.reshape(BLK // 2, 2, LANES)
             rest = pltpu.roll(rests[i // per_tile], -i % per_tile * BLK, 1)
             row = jnp.sum(jnp.where(mine, rest, 0.0), axis=0, keepdims=True)
@@ -229,7 +229,7 @@
     messages = call(
         pack_kernel,
         bf16(n_enc, PAIRS, 2, LANES),
-        [pltpu.VMEM((pix.shape[1], TILES * LANES), jnp.bfloat16)],
+        [],
         (me, counts, pix),
         None,
     )

time: 140 us -> 140 us (level)
  no operation moved by 1% of the time
where the time goes in v7:
time: 140 us; the launch traced here: 139 us
  blocking collectives  72.2 us (52%)
  starting transfers between devices  38.3 us (27%)
  waiting for transfers between devices  16.8 us (12%)
  Pallas kernels  11.5 us (8%)
    all_to_all x3, blocking collectives, exchange(): return lax.all_to_all(value, axes, split_axis=0, concat_axis=0, tiled=True)  72.2 us
    all_to_all x1, starting transfers between devices, exchange(): return lax.all_to_all(value, axes, split_axis=0, concat_axis=0, tiled=True)  23.8 us
    ppermute x4, starting transfers between devices, shift(): lax.ppermute(value, axis, [(i, (i + by) % size) for i in range(size)])  14.6 us
    pallas_call x6, Pallas kernels, call(): pl.pallas_call(kernel, out_shape=out_shape, in_specs=[pl.BlockSpec(memory...  11.5 us
    ppermute x4, waiting for transfers between devices, shift(): lax.ppermute(value, axis, [(i, (i + by) % size) for i in range(size)])  10.7 us
    all_to_all x1, waiting for transfers between devices, exchange(): return lax.all_to_all(value, axes, split_axis=0, concat_axis=0, tiled=True)  6.17 us
  transfers between devices with their start and end apart: 5, of which 4 were waited for; matrix products, arithmetic and copies ran while one was open for 0% of the time, Pallas kernels for 4%

profile of v7, /device:TPU:1, one launch (start us, length us, event | category | flops | bytes accessed | tf_op | source)
XLA Modules:
  0.0 139.2 jit_solution(8434382555496196381)
XLA Ops:
  0.0 0.0 copy-start.1
  0.0 0.0 copy-start
  0.0 2.9 %shard_map.38 = bf16[64,25,2,128]{3,2,1,0:T(2,128)(2,1)} custom-call(s32[1]{0:T(128)} %bitcast.me_ref, s32[1,64]{1,0:T(1,128)} %counts_ref.1, bf16[392,768]{1,0:T(8,128)(2,1)} %bitcast.13), custom_call_target="tpu_custom_call" | custom-call | bytes 6291456 | tf_op jit(solution)/shard_map/pallas_call | solution.py:206
  2.9 23.8 %all-to-all-start = ((bf16[64,25,2,128]{3,2,1,0:T(2,128)(2,1)}), bf16[64,25,2,128]{3,2,1,0:T(2,128)(2,1)S(1)}, u32[]{:S(2)}, u32[]{:S(2)}) async-start(bf16[64,25,2,128]{3,2,1,0:T(2,128)(2,1)} %shard_map.38), calls=%async_computation | async-start | bytes 1638400 | tf_op jit(solution)/shard_map/all_to_all | solution.py:192
  26.7 0.0 copy-done.1
  26.7 0.1 pad_add_fusion.at_ref
  26.8 0.0 copy-done
  26.8 2.3 %shard_map.40 = (bf16[2,256,384]{2,1,0:T(8,128)(2,1)S(1)}, bf16[2,256,384]{2,1,0:T(8,128)(2,1)}, bf16[2,256,384]{2,1,0:T(8,128)(2,1)S(1)}, bf16[2,256,384]{2,1,0:T(8,128)(2,1)S(1)}) custom-call(s32[67]{0:T(128)S(1)} %pad_add_fusion.at_ref, bf16[1728,384]{1,0:T(8,128)(2,1)S(1)} %bitcast.11), custom_call_target="tpu_custom_call" | custom-call | bytes 6291456 | tf_op jit(solution)/shard_map/pallas_call | solution.py:206
  29.1 2.9 %collective-permute-start = (bf16[2,256,384]{2,1,0:T(8,128)(2,1)}, bf16[2,256,384]{2,1,0:T(8,128)(2,1)S(1)}, u32[]{:S(2)}, u32[]{:S(2)}) collective-permute-start(bf16[2,256,384]{2,1,0:T(8,128)(2,1)} %get-tuple-element.17), channel_id=1, source_target_pairs={{0,1},{1,2},{2,3},{3,0},{4,5},{5,6},{6,7},{7,4},{8,9},{9,10},{10,1... | collective-permute-start | bytes 1179656 | tf_op jit(solution)/shard_map/ppermute | solution.py:197
  32.0 4.3 %collective-permute-start.1 = (bf16[2,256,384]{2,1,0:T(8,128)(2,1)S(1)}, bf16[2,256,384]{2,1,0:T(8,128)(2,1)S(1)}, u32[]{:S(2)}, u32[]{:S(2)}) collective-permute-start(bf16[2,256,384]{2,1,0:T(8,128)(2,1)S(1)} %get-tuple-element.18), channel_id=1, source_target_pairs={{0,2},{1,3},{2,0},{3,1},{4,6},{5,7},{6,4},{7,5},{8,10},{9,11},{10,... | collective-permute-start | bytes 1179656 | tf_op jit(solution)/shard_map/ppermute | solution.py:197
  36.3 3.1 %collective-permute-start.2 = (bf16[2,256,384]{2,1,0:T(8,128)(2,1)S(1)}, bf16[2,256,384]{2,1,0:T(8,128)(2,1)S(1)}, u32[]{:S(2)}, u32[]{:S(2)}) collective-permute-start(bf16[2,256,384]{2,1,0:T(8,128)(2,1)S(1)} %get-tuple-element.19), channel_id=1, source_target_pairs={{0,3},{1,0},{2,1},{3,2},{4,7},{5,4},{6,5},{7,6},{8,11},{9,8},{10,9... | collective-permute-start | bytes 1179656 | tf_op jit(solution)/shard_map/ppermute | solution.py:197
  39.4 2.4 %shard_map.37.from_ref = s32[24]{0:T(128)S(1)} custom-call(s32[67]{0:T(128)S(1)} %pad_add_fusion.at_ref), custom_call_target="tpu_custom_call" | custom-call | bytes 6291456 | tf_op jit(solution)/shard_map/pallas_call | solution.py:206
  41.8 6.2 %all-to-all-done.arrived_ref = bf16[64,25,2,128]{3,2,1,0:T(2,128)(2,1)S(1)} async-done(((bf16[64,25,2,128]{3,2,1,0:T(2,128)(2,1)}), bf16[64,25,2,128]{3,2,1,0:T(2,128)(2,1)S(1)}, u32[]{:S(2)}, u32[]{:S(2)}) %all-to-all-start) | async-done | bytes 819232 | tf_op jit(solution)/shard_map/all_to_all | solution.py:192
  48.0 1.0 shard_map.39
  49.0 0.0 collective-permute-done.refs_1_
  49.0 9.0 %collective-permute-done.1.refs_2_ = bf16[2,256,384]{2,1,0:T(8,128)(2,1)S(1)} collective-permute-done((bf16[2,256,384]{2,1,0:T(8,128)(2,1)S(1)}, bf16[2,256,384]{2,1,0:T(8,128)(2,1)S(1)}, u32[]{:S(2)}, u32[]{:S(2)}) %collective-permute-start.1) | collective-permute-done | bytes 393248 | tf_op jit(solution)/shard_map/ppermute | solution.py:197
  58.0 0.3 collective-permute-done.2.refs_3_
  58.3 19.6 %all_to_all.20.refs_4_ = bf16[4,400,384]{2,1,0:T(8,128)(2,1)S(1)} all-to-all(bf16[4,400,384]{2,1,0:T(8,128)(2,1)S(1)} %shard_map.39), channel_id=1, replica_groups=mesh['zl'=6,'core'=2,'zh'=2,'y'=8,'x'=4] {'x'}, dimensions={0} | all-to-all | bytes 2457600 | tf_op jit(solution)/shard_map/all_to_all | solution.py:192
  77.9 2.2 %shard_map.41 = (f32[8,96,128]{2,1,0:T(8,128)S(1)}, f32[8,96,128]{2,1,0:T(8,128)S(1)}) custom-call(s32[67]{0:T(128)S(1)} %pad_add_fusion.at_ref, bf16[2,256,384]{2,1,0:T(8,128)(2,1)S(1)} %get-tuple-element.20.refs_0_, bf16[2,256,384]{2,1,0:T(8,128)(2,1)S(1)} %collective-permute-done.refs_1_, bf16[2,256,384]{2,1,0:T(8,128)(2,1)S(1)} %collective-permute-done.1.refs_2_, ...), custom_call_target="tpu_custom_call" | custom-call | bytes 6291456 | tf_op jit(solution)/shard_map/pallas_call | solution.py:206
  80.1 4.3 %collective-permute-start.3 = (f32[8,96,128]{2,1,0:T(8,128)S(1)}, f32[8,96,128]{2,1,0:T(8,128)S(1)}, u32[]{:S(2)}, u32[]{:S(2)}) collective-permute-start(f32[8,96,128]{2,1,0:T(8,128)S(1)} %get-tuple-element.26), channel_id=1, source_target_pairs={{0,64},{64,0},{1,65},{65,1},{2,66},{66,2},{3,67},{67,3},{4,68},{68... | collective-permute-start | bytes 1179656 | tf_op jit(solution)/shard_map/ppermute | solution.py:197
  84.3 1.3 collective-permute-done.3
  85.7 0.1 add.13
  85.7 37.6 %all_to_all.21 = f32[96,8,128]{2,1,0:T(8,128)S(1)} all-to-all(f32[96,8,128]{2,1,0:T(8,128)S(1)} %bitcast.12), channel_id=1, replica_groups=mesh['zl'=6,'core'=2,'zh'=2,'y'=8,'x'=4] {'y','zh','zl'}, dimensions={0} | all-to-all | bytes 786432 | tf_op jit(solution)/shard_map/all_to_all | solution.py:192
  123.3 0.1 reduce_sum.9
  123.4 15.0 %all_to_all.22.parts_ref = f32[12,8,128]{2,1,0:T(8,128)S(1)} all-to-all(f32[12,8,128]{2,1,0:T(8,128)S(1)} %broadcast_in_dim.4), channel_id=1, replica_groups=mesh['zl'=6,'core'=2,'zh'=2,'y'=8,'x'=4] {'zl','core'}, dimensions={0} | all-to-all | bytes 98304 | tf_op jit(solution)/shard_map/all_to_all | solution.py:192
  138.4 0.7 shard_map.42
  (1 shorter events, 0.0 us)
Async XLA Ops:
  0.0 26.7 %copy-start.1 = (s32[1,64]{1,0:T(1,128)S(1)}, s32[1,64]{1,0:T(1,128)}, u32[]{:S(2)}) copy-start(s32[1,64]{1,0:T(1,128)} %counts_ref.1) | copy-start | bytes 772
  0.0 26.8 %copy-start = (bf16[1,384,1728]{1,2,0:T(8,128)(2,1)S(1)}, bf16[1,384,1728]{1,2,0:T(8,128)(2,1)}, u32[]{:S(2)}) copy-start(bf16[1,384,1728]{1,2,0:T(8,128)(2,1)} %param.5) | copy-start | bytes 3981316
  2.9 45.1 %all-to-all-start = ((bf16[64,25,2,128]{3,2,1,0:T(2,128)(2,1)}), bf16[64,25,2,128]{3,2,1,0:T(2,128)(2,1)S(1)}, u32[]{:S(2)}, u32[]{:S(2)}) async-start(bf16[64,25,2,128]{3,2,1,0:T(2,128)(2,1)} %shard_map.38), calls=%async_computation | async-start | bytes 1638400 | tf_op jit(solution)/shard_map/all_to_all | solution.py:192
  29.1 20.0 %collective-permute-start = (bf16[2,256,384]{2,1,0:T(8,128)(2,1)}, bf16[2,256,384]{2,1,0:T(8,128)(2,1)S(1)}, u32[]{:S(2)}, u32[]{:S(2)}) collective-permute-start(bf16[2,256,384]{2,1,0:T(8,128)(2,1)} %get-tuple-element.17), channel_id=1, source_target_pairs={{0,1},{1,2},{2,3},{3,0},{4,5},{5,6},{6,7},{7,4},{8,9},{9,10},{10,1... | collective-permute-start | bytes 1179656 | tf_op jit(solution)/shard_map/ppermute | solution.py:197
  32.0 26.1 %collective-permute-start.1 = (bf16[2,256,384]{2,1,0:T(8,128)(2,1)S(1)}, bf16[2,256,384]{2,1,0:T(8,128)(2,1)S(1)}, u32[]{:S(2)}, u32[]{:S(2)}) collective-permute-start(bf16[2,256,384]{2,1,0:T(8,128)(2,1)S(1)} %get-tuple-element.18), channel_id=1, source_target_pairs={{0,2},{1,3},{2,0},{3,1},{4,6},{5,7},{6,4},{7,5},{8,10},{9,11},{10,... | collective-permute-start | bytes 1179656 | tf_op jit(solution)/shard_map/ppermute | solution.py:197
  36.3 22.1 %collective-permute-start.2 = (bf16[2,256,384]{2,1,0:T(8,128)(2,1)S(1)}, bf16[2,256,384]{2,1,0:T(8,128)(2,1)S(1)}, u32[]{:S(2)}, u32[]{:S(2)}) collective-permute-start(bf16[2,256,384]{2,1,0:T(8,128)(2,1)S(1)} %get-tuple-element.19), channel_id=1, source_target_pairs={{0,3},{1,0},{2,1},{3,2},{4,7},{5,4},{6,5},{7,6},{8,11},{9,8},{10,9... | collective-permute-start | bytes 1179656 | tf_op jit(solution)/shard_map/ppermute | solution.py:197
  80.1 5.6 %collective-permute-start.3 = (f32[8,96,128]{2,1,0:T(8,128)S(1)}, f32[8,96,128]{2,1,0:T(8,128)S(1)}, u32[]{:S(2)}, u32[]{:S(2)}) collective-permute-start(f32[8,96,128]{2,1,0:T(8,128)S(1)} %get-tuple-element.26), channel_id=1, source_target_pairs={{0,64},{64,0},{1,65},{65,1},{2,66},{66,2},{3,67},{67,3},{4,68},{68... | collective-permute-start | bytes 1179656 | tf_op jit(solution)/shard_map/ppermute | solution.py:197
